TPU v7x, 128 devices: a whole 4x4x4 slice. The times are simulated.
128 devices in a mesh: gcm: 8 (over y, core), crm: 16 (over x, z).
Axes of the slice: x: 4, y: 4, z: 4, core: 2. Of those that a mesh axis runs over, the one named last changes fastest.
Arguments:
- tracer: float32 [72, 64, 4096], P(None, 'gcm', 'crm'), may hold values from -6 to 6
- wind_x: float32 [72, 64, 4096], P(None, 'gcm', 'crm'), may hold values from -4 to 4
- wind_y: float32 [72, 64, 4096], P(None, 'gcm', 'crm'), may hold values from -4 to 4
- drops: bfloat16 [16384, 33, 256], P(('gcm', 'crm')), may hold values from 0 to 1
- owner: int32 [16384, 1], P(('gcm', 'crm')), may hold values from 0 to 127, as said below
- counts: int32 [16384], P(('gcm', 'crm')), may hold values from 0 to 4, as said below
- collision: bfloat16 [33, 1089], replicated, may hold values from -0.1875 to 0.1875
- growth: float32 [33], replicated, may hold values from -4 to 4
Outputs:
- tracer_next: float32 [72, 64, 4096], P(None, 'gcm', 'crm')
- drops_next: bfloat16 [16384, 33, 256], P(('gcm', 'crm'))
- power: float32 [16, 32768], P(None, ('gcm', 'crm'))
Inputs may be any that keep to these rules, and one draw needn't show every extreme that they name: Owner index in gcm-then-crm device order; among the 128 columns of one device no owner appears more than 2 times, and some owner appears exactly 2 times. `counts`: how cloudy the columns are differs from device to device.
All inputs are finite; a program needn't handle non-finite values.
Results may differ from a plain program's by a relative error of at most 0.0018.
Values may be sent and summed in bfloat16 or wider, within the bound.
A program may use at most 128 MiB of HBM per device.

v0:
```python
import jax
import jax.numpy as jnp
import numpy as np
from jax import lax
from jax.sharding import PartitionSpec as P

CRM_X = 16
CRM_LEV = 16
DYN_STEPS = 2
SLOT_BLOCK = 16


DT_DYN = 0.04
DT_CRM = 0.05
DT_PHYS = 0.5
HIGH = lax.Precision.HIGHEST


def with_halo(block, sides, width):
    for axis, dim in sides:
        count = lax.axis_size(axis)
        forward = [(i, i + 1) for i in range(count - 1)]
        forward.append((count - 1, 0))
        backward = [(target, source) for source, target in forward]
        low = lax.ppermute(
            lax.slice_in_dim(block, block.shape[dim] - width, None, axis=dim), axis, forward
        )
        high = lax.ppermute(lax.slice_in_dim(block, 0, width, axis=dim), axis, backward)
        block = jnp.concatenate([low, block, high], axis=dim)
    return block


def gll_tables():
    inv_root = 1.0 / np.sqrt(5.0)
    gll_nodes = np.array([-1.0, -inv_root, inv_root, 1.0])
    weights = np.array([1.0, 5.0, 5.0, 1.0]) / 6.0
    legendre = (5.0 * gll_nodes**3 - 3.0 * gll_nodes) / 2.0
    derivative = np.zeros((4, 4))
    for i in range(4):
        for j in range(4):
            if i != j:
                derivative[i, j] = legendre[i] / (legendre[j] * (gll_nodes[i] - gll_nodes[j]))
    derivative[0, 0] = -3.0
    derivative[3, 3] = 3.0
    return (2.0 * derivative, weights)


def level_tables(levels, crm_levels):
    spacing = levels / crm_levels
    centres = (np.arange(crm_levels) + 0.5) * spacing - 0.5
    hats = np.maximum(0.0, 1.0 - np.abs(np.arange(levels)[None, :] - centres[:, None]) / spacing)
    down_map = hats / hats.sum(axis=1, keepdims=True)
    up_map = hats.T / hats.T.sum(axis=1, keepdims=True)
    return (down_map, up_map)


def sum_rows(padded):
    row_count = padded.shape[1] - 2
    phase = (jnp.arange(row_count) % 4)[None, :, None]
    middle = padded[:, 1:-1]
    return (
        middle
        + jnp.where(phase == 3, padded[:, 2:], 0.0)
        + jnp.where(phase == 0, padded[:, :-2], 0.0)
    )


def sum_cols(padded):
    col_count = padded.shape[2] - 2
    phase = (jnp.arange(col_count) % 4)[None, None, :]
    middle = padded[:, :, 1:-1]
    return (
        middle
        + jnp.where(phase == 3, padded[:, :, 2:], 0.0)
        + jnp.where(phase == 0, padded[:, :, :-2], 0.0)
    )


def assemble(field, mass_pattern, denominator):
    weighted = field * mass_pattern
    along_rows = sum_rows(with_halo(weighted, (("gcm", 1),), 1))
    summed = sum_cols(with_halo(along_rows, (("crm", 2),), 1))
    return summed / denominator


def advect(tracer, wind_x, wind_y, derivative):
    levels, row_count, col_count = tracer.shape
    by_rows = tracer.reshape(levels, row_count // 4, 4, col_count)
    grad_x = jnp.einsum("ij,lejc->leic", derivative, by_rows, precision=HIGH).reshape(tracer.shape)
    by_cols = tracer.reshape(levels, row_count, col_count // 4, 4)
    grad_y = jnp.einsum("ij,lrej->lrei", derivative, by_cols, precision=HIGH).reshape(tracer.shape)
    return -(wind_x * grad_x + wind_y * grad_y)


def crm_substep(state, cell_forcing, growth, collision):
    grown = state + DT_CRM * cell_forcing[:, None, :] * growth[None, :, None]
    slot_count, bin_count, cell_count = grown.shape
    pairs = (grown[:, :, None, :] * grown[:, None, :, :]).reshape(
        slot_count, bin_count * bin_count, cell_count
    )
    change = jnp.einsum(
        "kq,sqc->skc", collision, pairs.astype(jnp.bfloat16), preferred_element_type=jnp.float32
    )
    return grown + DT_CRM * change


def summarize(final, initial):
    slot_count, bin_count, cell_count = final.shape
    mass = (jnp.arange(bin_count).astype(final.dtype) + 1.0) / bin_count
    heat = jnp.einsum("b,sbc->sc", mass, final - initial, precision=HIGH)
    echo = jnp.einsum("b,sbc->sc", mass * mass, final * final, precision=HIGH)
    heat = heat.reshape(slot_count, cell_count // CRM_X, CRM_X).mean(axis=2)
    echo = echo.reshape(slot_count, cell_count // CRM_X, CRM_X).mean(axis=2)
    return (heat, jnp.log(1.0 + echo))


def run_slots(drops, forcing, counts, collision, growth):
    slot_count = drops.shape[0]
    nblock = slot_count // SLOT_BLOCK
    ordering = jnp.argsort(-counts, stable=True)
    restore = jnp.argsort(ordering, stable=True)
    sorted_drops = jnp.take(drops, ordering, axis=0)
    sorted_forcing = jnp.take(forcing, ordering, axis=0)
    sorted_counts = jnp.take(counts, ordering, axis=0)

    def run_block(block):
        block_drops, block_forcing, block_counts = block
        initial = block_drops.astype(jnp.float32)
        cell_forcing = jnp.repeat(block_forcing.astype(jnp.float32), CRM_X, axis=1)

        def advance(step, current):
            moved = crm_substep(current, cell_forcing, growth, collision)
            return jnp.where((step < block_counts)[:, None, None], moved, current)

        final = lax.fori_loop(0, jnp.max(block_counts), advance, initial)
        heat, echo_power = summarize(final, initial)
        return (final.astype(jnp.bfloat16), heat.astype(jnp.bfloat16), echo_power)

    finals, heats, powers = lax.map(
        run_block,
        (
            sorted_drops.reshape((nblock, SLOT_BLOCK) + drops.shape[1:]),
            sorted_forcing.reshape((nblock, SLOT_BLOCK) + forcing.shape[1:]),
            sorted_counts.reshape(nblock, SLOT_BLOCK),
        ),
    )
    finals = jnp.take(finals.reshape(drops.shape), restore, axis=0)
    heats = jnp.take(heats.reshape(forcing.shape), restore, axis=0)
    powers = jnp.take(powers.reshape(forcing.shape), restore, axis=0)
    return (finals, heats, powers)


def buffer_sources(slot_of, slot_total):
    col_total = slot_of.shape[0]
    marks = (
        jnp.zeros((slot_total,), jnp.int32)
        .at[slot_of]
        .set(jnp.arange(1, col_total + 1, dtype=jnp.int32))
    )
    return (jnp.maximum(marks - 1, 0), marks > 0)


def pack_rows(values, pick, filled):
    taken = jnp.take(values, pick, axis=0)
    shaped_mask = filled.reshape(filled.shape + (1,) * (values.ndim - 1))
    return jnp.where(shaped_mask, taken, jnp.zeros((), values.dtype))


def shards(tracer, wind_x, wind_y, drops, owner, counts, collision, growth):
    n_gcm = lax.axis_size("gcm")
    n_crm = lax.axis_size("crm")
    devices = n_gcm * n_crm
    levels, row_count, col_count = tracer.shape
    derivative, gll_weights = gll_tables()
    derivative = jnp.asarray(derivative, tracer.dtype)
    gll_weights = jnp.asarray(gll_weights, tracer.dtype)
    mass_pattern = jnp.outer(
        jnp.tile(gll_weights, row_count // 4), jnp.tile(gll_weights, col_count // 4)
    )[None]
    denominator = sum_cols(sum_rows(jnp.pad(mass_pattern, ((0, 0), (1, 1), (1, 1)), mode="wrap")))
    state = tracer
    for step in range(DYN_STEPS):
        state = state + DT_DYN * assemble(
            advect(state, wind_x, wind_y, derivative), mass_pattern, denominator
        )
    blocks = ((state - tracer) / (DYN_STEPS * DT_DYN)).reshape(
        levels, row_count // 4, 4, col_count // 4, 4
    )
    means = jnp.einsum("laibj,i,j->abl", blocks, gll_weights, gll_weights, precision=HIGH) / 4.0
    col_total = drops.shape[0]
    means = means.reshape(col_total, levels)
    down_map, up_map = level_tables(levels, CRM_LEV)
    forcing = jnp.dot(means, jnp.asarray(down_map.T, jnp.float32), precision=HIGH).astype(
        jnp.bfloat16
    )
    capacity = 2 * col_total // devices
    slot_total = devices * capacity
    owners = owner[:, 0]
    onehot = (owners[:, None] == jnp.arange(devices, dtype=jnp.int32)[None, :]).astype(jnp.int32)
    earlier = jnp.cumsum(onehot, axis=0) - onehot
    slot_of = owners * capacity + jnp.sum(earlier * onehot, axis=1)
    pick, filled = buffer_sources(slot_of, slot_total)
    send_drops = pack_rows(drops, pick, filled)
    send_forcing = pack_rows(forcing, pick, filled)
    send_counts = pack_rows(counts, pick, filled).astype(jnp.bfloat16)
    got_drops, got_forcing, got_counts = (
        lax.all_to_all(send_drops, ("gcm", "crm"), split_axis=0, concat_axis=0, tiled=True),
        lax.all_to_all(send_forcing, ("gcm", "crm"), split_axis=0, concat_axis=0, tiled=True),
        lax.all_to_all(send_counts, ("gcm", "crm"), split_axis=0, concat_axis=0, tiled=True),
    )
    finals, heats, echo_power = run_slots(
        got_drops, got_forcing, got_counts.astype(jnp.int32), collision, growth
    )
    back_drops, back_heat = (
        lax.all_to_all(finals, ("gcm", "crm"), split_axis=0, concat_axis=0, tiled=True),
        lax.all_to_all(heats, ("gcm", "crm"), split_axis=0, concat_axis=0, tiled=True),
    )
    drops_next = jnp.take(back_drops, slot_of, axis=0)
    heat = jnp.take(back_heat, slot_of, axis=0).astype(jnp.float32)
    power = echo_power.T
    back = jnp.dot(heat, jnp.asarray(up_map.T, jnp.float32), precision=HIGH)
    grid = back.T.reshape(levels, row_count // 4, 1, col_count // 4, 1)
    spread = jnp.broadcast_to(grid, (levels, row_count // 4, 4, col_count // 4, 4)).reshape(
        tracer.shape
    )
    tracer_next = assemble(state + DT_PHYS * spread, mass_pattern, denominator)
    return (tracer_next, drops_next, power)


def solution(mesh):
    return jax.shard_map(
        shards,
        mesh=mesh,
        in_specs=(
            P(None, "gcm", "crm"),
            P(None, "gcm", "crm"),
            P(None, "gcm", "crm"),
            P(("gcm", "crm"), None, None),
            P(("gcm", "crm"), None),
            P(("gcm", "crm")),
            P(),
            P(),
        ),
        out_specs=(P(None, "gcm", "crm"), P(("gcm", "crm"), None, None), P(None, ("gcm", "crm"))),
        check_vma=False,
    )
```

profile of v0, /device:TPU:0, one launch (start us, length us, event | category | flops | bytes accessed | tf_op | source)
XLA Modules:
  0.0 487.1 jit_solution(10035945381557932126)
XLA Ops:
  34.0 6.2 %collective-permute-start.2 = (f32[72,8,1]{0,1,2:T(8,128)S(1)}, f32[72,8,1]{0,1,2:T(8,128)S(1)}, u32[]{:S(2)}, u32[]{:S(2)}) collective-permute-start(f32[72,8,1]{0,1,2:T(8,128)S(1)} %get-tuple-element.178), channel_id=1, source_target_pairs={{1,0},{2,1},{3,2},{4,3},{5,4},{6,5},{7,6},{8,7},{9,8},{10,9},{11,1... | collective-permute-start | bytes 6920 | tf_op jit(solution)/shard_map/ppermute | solution.py:28
  43.0 4.3 collective-permute-done.3
  66.9 4.9 all-to-all-start.1
  75.5 5.0 %collective-permute-start.6 = (f32[72,8,1]{0,1,2:T(8,128)S(1)}, f32[72,8,1]{0,1,2:T(8,128)S(1)}, u32[]{:S(2)}, u32[]{:S(2)}) collective-permute-start(f32[72,8,1]{0,1,2:T(8,128)S(1)} %get-tuple-element.174), channel_id=1, source_target_pairs={{1,0},{2,1},{3,2},{4,3},{5,4},{6,5},{7,6},{8,7},{9,8},{10,9},{11,1... | collective-permute-start | bytes 6920 | tf_op jit(solution)/shard_map/ppermute | solution.py:28
  82.5 15.6 %gather_fusion = bf16[256,33,256]{2,0,1:T(8,128)(2,1)} fusion(bf16[128,33,256]{2,0,1:T(8,128)(2,1)S(1)} %copy-done, s32[1024]{0:T(1024)S(1)} %pad_clamp_fusion.3), kind=kCustom, calls=%fused_computation.4 | custom fusion | bytes 8651776 | tf_op jit(solution)/shard_map/jit(_take)/gather | solution.py:164
  105.3 9.8 %all-to-all-start.2 = ((bf16[128,2,16]{2,1,0:T(2,128)(2,1)}), bf16[128,2,16]{2,1,0:T(2,128)(2,1)S(1)}, u32[]{:S(2)}, u32[]{:S(2)}) async-start(bf16[128,2,16]{2,1,0:T(2,128)(2,1)} %broadcast_select_fusion.4), calls=%async_computation.2 | async-start | bytes 131072 | tf_op jit(solution)/shard_map/all_to_all | solution.py:208
  118.4 4.8 copy.110
  124.5 9.1 %all-to-all-start = ((bf16[256,33,256]{2,1,0:T(8,128)(2,1)}), bf16[256,33,256]{2,1,0:T(8,128)(2,1)}, u32[]{:S(2)}, u32[]{:S(2)}) async-start(bf16[256,33,256]{2,1,0:T(8,128)(2,1)} %copy.110), calls=%async_computation | async-start | bytes 10485760 | tf_op jit(solution)/shard_map/all_to_all | solution.py:207
  144.5 51.9 %all-to-all-done = bf16[256,33,256]{2,1,0:T(8,128)(2,1)} async-done(((bf16[256,33,256]{2,1,0:T(8,128)(2,1)}), bf16[256,33,256]{2,1,0:T(8,128)(2,1)}, u32[]{:S(2)}, u32[]{:S(2)}) %all-to-all-start) | async-done | bytes 4325408 | tf_op jit(solution)/shard_map/all_to_all | solution.py:207
  196.4 5.7 %gather_fusion.7 = bf16[256,33,256]{2,1,0:T(8,128)(2,1)} fusion(bf16[256,33,256]{2,1,0:T(8,128)(2,1)} %all-to-all-done, s32[1024]{0:T(1024)S(1)} %pad_clamp_fusion.2), kind=kCustom, calls=%fused_computation.clone | custom fusion | bytes 8651776 | tf_op jit(solution)/shard_map/jit(_take)/gather | solution.py:122
  202.1 5.4 %broadcast_select_fusion.1 = bf16[256,33,256]{2,1,0:T(8,128)(2,1)} fusion(bf16[256,33,256]{2,1,0:T(8,128)(2,1)} %gather_fusion.7, pred[256]{0:T(512)(128)(4,1)S(1)} %get-tuple-element.164), kind=kLoop, calls=%fused_computation.54 | loop fusion | flops 2162688 | bytes 8651008 | tf_op jit(solution)/shard_map/jit(_take)/select_n | solution.py:122
  207.5 134.6 %while.26 = (s32[]{:T(128)}, bf16[16,16,33,256]{3,2,1,0:T(8,128)(2,1)}, bf16[16,16,16]{2,1,0:T(8,128)(2,1)S(1)}, f32[16,16,16]{2,1,0:T(8,128)S(1)}, bf16[16,16,3...) while((s32[]{:T(128)}, ...), condition=%wide.region_10.13_spmd, body=%wide.region_4.12_spmd.sunk | while | flops 308192544 | bytes 25102840 | solution.py:139
  209.2 26.1 %while.27 = (s32[]{:T(128)}, f32[16,33,256]{2,1,0:T(8,128)S(1)}, s32[]{:T(128)}, s32[16]{0:T(128)S(1)}, f32[33]{0:T(128)S(1)}, /*index=5*/bf16[33,1089]{1,0:T(8,128)(2,1)S(1)}, f32[16,16]{1,0:T(8,128)S(1)}, s32[]{:T(128)}) while((s32[]{:T(128)}, f32[16,33,256]{2,1,0:T(8,128)S(1)}, s32[]{:T(128)}, s32[16]{0:T(128)S(1)}, ...), condition=%wide.region_7.9_spmd.clone, body=%wide.region_6.8_spmd.clone.sunk | while | flops 304263456 | bytes 21784196 | solution.py:135
  240.3 7.0 %while.27 = (s32[]{:T(128)}, f32[16,33,256]{2,1,0:T(8,128)S(1)}, s32[]{:T(128)}, s32[16]{0:T(128)S(1)}, f32[33]{0:T(128)S(1)}, /*index=5*/bf16[33,1089]{1,0:T(8,128)(2,1)S(1)}, f32[16,16]{1,0:T(8,128)S(1)}, s32[]{:T(128)}) while((s32[]{:T(128)}, f32[16,33,256]{2,1,0:T(8,128)S(1)}, s32[]{:T(128)}, s32[16]{0:T(128)S(1)}, ...), condition=%wide.region_7.9_spmd.clone, body=%wide.region_6.8_spmd.clone.sunk | while | flops 304263456 | bytes 21784196 | solution.py:135
  252.3 7.0 %while.27 = (s32[]{:T(128)}, f32[16,33,256]{2,1,0:T(8,128)S(1)}, s32[]{:T(128)}, s32[16]{0:T(128)S(1)}, f32[33]{0:T(128)S(1)}, /*index=5*/bf16[33,1089]{1,0:T(8,128)(2,1)S(1)}, f32[16,16]{1,0:T(8,128)S(1)}, s32[]{:T(128)}) while((s32[]{:T(128)}, f32[16,33,256]{2,1,0:T(8,128)S(1)}, s32[]{:T(128)}, s32[16]{0:T(128)S(1)}, ...), condition=%wide.region_7.9_spmd.clone, body=%wide.region_6.8_spmd.clone.sunk | while | flops 304263456 | bytes 21784196 | solution.py:135
  264.3 7.0 %while.27 = (s32[]{:T(128)}, f32[16,33,256]{2,1,0:T(8,128)S(1)}, s32[]{:T(128)}, s32[16]{0:T(128)S(1)}, f32[33]{0:T(128)S(1)}, /*index=5*/bf16[33,1089]{1,0:T(8,128)(2,1)S(1)}, f32[16,16]{1,0:T(8,128)S(1)}, s32[]{:T(128)}) while((s32[]{:T(128)}, f32[16,33,256]{2,1,0:T(8,128)S(1)}, s32[]{:T(128)}, s32[16]{0:T(128)S(1)}, ...), condition=%wide.region_7.9_spmd.clone, body=%wide.region_6.8_spmd.clone.sunk | while | flops 304263456 | bytes 21784196 | solution.py:135
  342.1 5.8 %gather_fusion.10 = bf16[256,33,256]{2,1,0:T(8,128)(2,1)} fusion(bf16[256,33,256]{2,1,0:T(8,128)(2,1)} %bitcast.134, s32[1024]{0:T(1024)S(1)} %copy-done.24), kind=kCustom, calls=%fused_computation.2.clone | custom fusion | bytes 8651776 | tf_op jit(solution)/shard_map/jit(_take)/gather | solution.py:147
  349.5 36.2 %all-to-all-start.3 = ((bf16[128,2,16]{2,1,0:T(2,128)(2,1)}), bf16[128,2,16]{2,1,0:T(2,128)(2,1)S(1)}, u32[]{:S(2)}, u32[]{:S(2)}) async-start(bf16[128,2,16]{2,1,0:T(2,128)(2,1)} %bitcast.39), calls=%async_computation.3 | async-start | bytes 131072 | tf_op jit(solution)/shard_map/all_to_all | solution.py:216
  385.7 5.4 %broadcast_select_fusion = bf16[256,33,256]{2,1,0:T(8,128)(2,1)} fusion(bf16[256,33,256]{2,1,0:T(8,128)(2,1)} %gather_fusion.10, pred[256]{0:T(512)(128)(4,1)S(1)} %copy-done.35), kind=kLoop, calls=%fused_computation.53 | loop fusion | flops 2162688 | bytes 8651008 | tf_op jit(solution)/shard_map/jit(_take)/select_n | solution.py:147
  395.1 6.6 %all-to-all-start.4 = ((bf16[256,33,256]{2,1,0:T(8,128)(2,1)}), bf16[256,33,256]{2,1,0:T(8,128)(2,1)}, u32[]{:S(2)}, u32[]{:S(2)}) async-start(bf16[256,33,256]{2,1,0:T(8,128)(2,1)} %broadcast_select_fusion), calls=%async_computation.4 | async-start | bytes 10485760 | tf_op jit(solution)/shard_map/all_to_all | solution.py:215
  409.9 51.1 %collective-permute-done.8 = f32[72,1,256]{0,1,2:T(1,128)S(1)} collective-permute-done((f32[72,1,256]{0,1,2:T(1,128)S(1)}, f32[72,1,256]{0,1,2:T(1,128)S(1)}, u32[]{:S(2)}, u32[]{:S(2)}) %collective-permute-start.8) | collective-permute-done | bytes 73760 | tf_op jit(solution)/shard_map/ppermute | solution.py:28
  463.1 5.1 %collective-permute-start.10 = (f32[72,8,1]{0,1,2:T(8,128)S(1)}, f32[72,8,1]{0,1,2:T(8,128)S(1)}, u32[]{:S(2)}, u32[]{:S(2)}) collective-permute-start(f32[72,8,1]{0,1,2:T(8,128)S(1)} %get-tuple-element.170), channel_id=1, source_target_pairs={{1,0},{2,1},{3,2},{4,3},{5,4},{6,5},{7,6},{8,7},{9,8},{10,9},{11,1... | collective-permute-start | bytes 6920 | tf_op jit(solution)/shard_map/ppermute | solution.py:28
  469.6 5.6 %collective-permute-done.11 = f32[72,8,1]{0,1,2:T(8,128)S(1)} collective-permute-done((f32[72,8,1]{0,1,2:T(8,128)S(1)}, f32[72,8,1]{0,1,2:T(8,128)S(1)}, u32[]{:S(2)}, u32[]{:S(2)}) %collective-permute-start.11) | collective-permute-done | bytes 2336 | tf_op jit(solution)/shard_map/ppermute | solution.py:25
  478.1 4.9 %gather_fusion.5 = bf16[128,33,256]{2,1,0:T(8,128)(2,1)} fusion(bf16[256,33,256]{2,1,0:T(8,128)(2,1)} %all-to-all-done.4, s32[1024]{0:T(1024)S(1)} %pad_clamp_fusion), kind=kCustom, calls=%fused_computation.9 | custom fusion | bytes 4325888 | tf_op jit(solution)/shard_map/jit(_take)/gather | solution.py:218
  (493 shorter events, 232.5 us)
Async XLA Ops:
  0.6 81.8 %copy-start = (bf16[128,33,256]{2,0,1:T(8,128)(2,1)S(1)}, bf16[128,33,256]{2,0,1:T(8,128)(2,1)}, u32[]{:S(2)}) copy-start(bf16[128,33,256]{2,0,1:T(8,128)(2,1)} %param.23) | copy-start | bytes 6488068
  23.0 5.4 %collective-permute-start = (f32[72,1,256]{0,1,2:T(1,128)}, f32[72,1,256]{0,1,2:T(1,128)}, u32[]{:S(2)}, u32[]{:S(2)}) collective-permute-start(f32[72,1,256]{0,1,2:T(1,128)} %get-tuple-element.180), channel_id=1, source_target_pairs={{16,0},{32,16},{48,32},{64,48},{80,64},{96,80},{112,96},{0,112},{1... | collective-permute-start | bytes 221192 | tf_op jit(solution)/shard_map/ppermute | solution.py:28
  25.5 5.9 %collective-permute-start.1 = (f32[72,1,256]{0,1,2:T(1,128)}, f32[72,1,256]{0,1,2:T(1,128)}, u32[]{:S(2)}, u32[]{:S(2)}) collective-permute-start(f32[72,1,256]{0,1,2:T(1,128)} %get-tuple-element.181), channel_id=1, source_target_pairs={{0,16},{16,32},{32,48},{48,64},{64,80},{80,96},{96,112},{112,0},{1... | collective-permute-start | bytes 221192 | tf_op jit(solution)/shard_map/ppermute | solution.py:25
  25.7 72.4 %copy-start.20 = (pred[256]{0:T(512)(128)(4,1)}, pred[256]{0:T(512)(128)(4,1)S(1)}, u32[]{:S(2)}) copy-start(pred[256]{0:T(512)(128)(4,1)S(1)} %get-tuple-element.188) | copy-start | bytes 772
  25.7 72.4 %copy-start.22 = (pred[256]{0:T(512)(128)(4,1)}, pred[256]{0:T(512)(128)(4,1)S(1)}, u32[]{:S(2)}) copy-start(pred[256]{0:T(512)(128)(4,1)S(1)} %get-tuple-element.189) | copy-start | bytes 772
  34.0 9.0 %collective-permute-start.2 = (f32[72,8,1]{0,1,2:T(8,128)S(1)}, f32[72,8,1]{0,1,2:T(8,128)S(1)}, u32[]{:S(2)}, u32[]{:S(2)}) collective-permute-start(f32[72,8,1]{0,1,2:T(8,128)S(1)} %get-tuple-element.178), channel_id=1, source_target_pairs={{1,0},{2,1},{3,2},{4,3},{5,4},{6,5},{7,6},{8,7},{9,8},{10,9},{11,1... | collective-permute-start | bytes 6920 | tf_op jit(solution)/shard_map/ppermute | solution.py:28
  40.2 7.1 %collective-permute-start.3 = (f32[72,8,1]{0,1,2:T(8,128)S(1)}, f32[72,8,1]{0,1,2:T(8,128)S(1)}, u32[]{:S(2)}, u32[]{:S(2)}) collective-permute-start(f32[72,8,1]{0,1,2:T(8,128)S(1)} %get-tuple-element.179), channel_id=1, source_target_pairs={{0,1},{1,2},{2,3},{3,4},{4,5},{5,6},{6,7},{7,8},{8,9},{9,10},{10,1... | collective-permute-start | bytes 6920 | tf_op jit(solution)/shard_map/ppermute | solution.py:25
  40.6 57.5 %copy-start.10 = (f32[1,8,256]{1,2,0:T(8,128)}, f32[1,8,256]{1,2,0:T(8,128)S(1)}, u32[]{:S(2)}) copy-start(f32[1,8,256]{1,2,0:T(8,128)S(1)} %copy.130) | copy-start | bytes 24580
  64.3 7.5 %collective-permute-start.4 = (f32[72,1,256]{0,1,2:T(1,128)}, f32[72,1,256]{0,1,2:T(1,128)S(1)}, u32[]{:S(2)}, u32[]{:S(2)}) collective-permute-start(f32[72,1,256]{0,1,2:T(1,128)} %get-tuple-element.176), channel_id=1, source_target_pairs={{16,0},{32,16},{48,32},{64,48},{80,64},{96,80},{112,96},{0,112},{1... | collective-permute-start | bytes 221192 | tf_op jit(solution)/shard_map/ppermute | solution.py:28
  64.3 7.5 %collective-permute-start.5 = (f32[72,1,256]{0,1,2:T(1,128)}, f32[72,1,256]{0,1,2:T(1,128)}, u32[]{:S(2)}, u32[]{:S(2)}) collective-permute-start(f32[72,1,256]{0,1,2:T(1,128)} %get-tuple-element.177), channel_id=1, source_target_pairs={{0,16},{16,32},{32,48},{48,64},{64,80},{80,96},{96,112},{112,0},{1... | collective-permute-start | bytes 221192 | tf_op jit(solution)/shard_map/ppermute | solution.py:25
  66.9 38.4 %all-to-all-start.1 = ((bf16[128,2,1]{1,2,0:T(2,128)(2,1)}), bf16[128,2,1]{1,2,0:T(2,128)(2,1)S(1)}, u32[]{:S(2)}, u32[]{:S(2)}) async-start(bf16[128,2,1]{1,2,0:T(2,128)(2,1)} %all_to_all.35), calls=%async_computation.1 | async-start | bytes 131072 | tf_op jit(solution)/shard_map/all_to_all | solution.py:209
  75.5 22.5 %collective-permute-start.6 = (f32[72,8,1]{0,1,2:T(8,128)S(1)}, f32[72,8,1]{0,1,2:T(8,128)S(1)}, u32[]{:S(2)}, u32[]{:S(2)}) collective-permute-start(f32[72,8,1]{0,1,2:T(8,128)S(1)} %get-tuple-element.174), channel_id=1, source_target_pairs={{1,0},{2,1},{3,2},{4,3},{5,4},{6,5},{7,6},{8,7},{9,8},{10,9},{11,1... | collective-permute-start | bytes 6920 | tf_op jit(solution)/shard_map/ppermute | solution.py:28
  80.5 17.5 %collective-permute-start.7 = (f32[72,8,1]{0,1,2:T(8,128)S(1)}, f32[72,8,1]{0,1,2:T(8,128)S(1)}, u32[]{:S(2)}, u32[]{:S(2)}) collective-permute-start(f32[72,8,1]{0,1,2:T(8,128)S(1)} %get-tuple-element.175), channel_id=1, source_target_pairs={{0,1},{1,2},{2,3},{3,4},{4,5},{5,6},{6,7},{7,8},{8,9},{9,10},{10,1... | collective-permute-start | bytes 6920 | tf_op jit(solution)/shard_map/ppermute | solution.py:25
  105.3 19.2 %all-to-all-start.2 = ((bf16[128,2,16]{2,1,0:T(2,128)(2,1)}), bf16[128,2,16]{2,1,0:T(2,128)(2,1)S(1)}, u32[]{:S(2)}, u32[]{:S(2)}) async-start(bf16[128,2,16]{2,1,0:T(2,128)(2,1)} %broadcast_select_fusion.4), calls=%async_computation.2 | async-start | bytes 131072 | tf_op jit(solution)/shard_map/all_to_all | solution.py:208
  124.5 71.9 %all-to-all-start = ((bf16[256,33,256]{2,1,0:T(8,128)(2,1)}), bf16[256,33,256]{2,1,0:T(8,128)(2,1)}, u32[]{:S(2)}, u32[]{:S(2)}) async-start(bf16[256,33,256]{2,1,0:T(8,128)(2,1)} %copy.110), calls=%async_computation | async-start | bytes 10485760 | tf_op jit(solution)/shard_map/all_to_all | solution.py:207
  207.5 134.6 %copy-start.24 = (s32[1024]{0:T(1024)S(1)}, s32[1024]{0:T(1024)}, u32[]{:S(2)}) copy-start(s32[1024]{0:T(1024)} %pad_clamp_fusion.1) | copy-start | bytes 12292
  349.5 45.6 %all-to-all-start.3 = ((bf16[128,2,16]{2,1,0:T(2,128)(2,1)}), bf16[128,2,16]{2,1,0:T(2,128)(2,1)S(1)}, u32[]{:S(2)}, u32[]{:S(2)}) async-start(bf16[128,2,16]{2,1,0:T(2,128)(2,1)} %bitcast.39), calls=%async_computation.3 | async-start | bytes 131072 | tf_op jit(solution)/shard_map/all_to_all | solution.py:216
  395.1 83.0 %all-to-all-start.4 = ((bf16[256,33,256]{2,1,0:T(8,128)(2,1)}), bf16[256,33,256]{2,1,0:T(8,128)(2,1)}, u32[]{:S(2)}, u32[]{:S(2)}) async-start(bf16[256,33,256]{2,1,0:T(8,128)(2,1)} %broadcast_select_fusion), calls=%async_computation.4 | async-start | bytes 10485760 | tf_op jit(solution)/shard_map/all_to_all | solution.py:215
  401.7 60.8 %copy-start.27 = (pred[8]{0:T(512)(128)(4,1)S(1)}, pred[8]{0:T(512)(128)(4,1)}, u32[]{:S(2)}) copy-start(pred[8]{0:T(512)(128)(4,1)} %copy-done.26) | copy-start | bytes 28
  401.7 60.8 %copy-start.29 = (pred[8]{0:T(512)(128)(4,1)S(1)}, pred[8]{0:T(512)(128)(4,1)}, u32[]{:S(2)}) copy-start(pred[8]{0:T(512)(128)(4,1)} %copy-done.28) | copy-start | bytes 28
  407.0 54.0 %collective-permute-start.8 = (f32[72,1,256]{0,1,2:T(1,128)S(1)}, f32[72,1,256]{0,1,2:T(1,128)S(1)}, u32[]{:S(2)}, u32[]{:S(2)}) collective-permute-start(f32[72,1,256]{0,1,2:T(1,128)S(1)} %get-tuple-element.172), channel_id=1, source_target_pairs={{16,0},{32,16},{48,32},{64,48},{80,64},{96,80},{112,96},{0,112},{1... | collective-permute-start | bytes 221192 | tf_op jit(solution)/shard_map/ppermute | solution.py:28
  409.2 53.4 %collective-permute-start.9 = (f32[72,1,256]{0,1,2:T(1,128)S(1)}, f32[72,1,256]{0,1,2:T(1,128)S(1)}, u32[]{:S(2)}, u32[]{:S(2)}) collective-permute-start(f32[72,1,256]{0,1,2:T(1,128)S(1)} %get-tuple-element.173), channel_id=1, source_target_pairs={{0,16},{16,32},{32,48},{48,64},{64,80},{80,96},{96,112},{112,0},{1... | collective-permute-start | bytes 221192 | tf_op jit(solution)/shard_map/ppermute | solution.py:25
  463.1 6.5 %collective-permute-start.10 = (f32[72,8,1]{0,1,2:T(8,128)S(1)}, f32[72,8,1]{0,1,2:T(8,128)S(1)}, u32[]{:S(2)}, u32[]{:S(2)}) collective-permute-start(f32[72,8,1]{0,1,2:T(8,128)S(1)} %get-tuple-element.170), channel_id=1, source_target_pairs={{1,0},{2,1},{3,2},{4,3},{5,4},{6,5},{7,6},{8,7},{9,8},{10,9},{11,1... | collective-permute-start | bytes 6920 | tf_op jit(solution)/shard_map/ppermute | solution.py:28
  468.2 6.9 %collective-permute-start.11 = (f32[72,8,1]{0,1,2:T(8,128)S(1)}, f32[72,8,1]{0,1,2:T(8,128)S(1)}, u32[]{:S(2)}, u32[]{:S(2)}) collective-permute-start(f32[72,8,1]{0,1,2:T(8,128)S(1)} %get-tuple-element.171), channel_id=1, source_target_pairs={{0,1},{1,2},{2,3},{3,4},{4,5},{5,6},{6,7},{7,8},{8,9},{9,10},{10,1... | collective-permute-start | bytes 6920 | tf_op jit(solution)/shard_map/ppermute | solution.py:25
  (33 other events, 449.7 us)
where the time goes:
time: 496 us; the launch traced here: 487 us
  waiting for transfers between devices  124 us (25%)
  other arithmetic  115 us (23%)
  starting transfers between devices  88.4 us (18%)
  local copies, waits for them, and re-layouts  80.1 us (16%)
  matrix products  60.8 us (12%)
  loops' own time  17.8 us (4%)
    ppermute x6, waiting for transfers between devices, with_halo(): lax.ppermute(lax.slice_in_dim(block, 0, width, axis=dim), axis, backward)  52 us
    all_to_all x1, waiting for transfers between devices, shards(): lax.all_to_all(send_drops, ('gcm', 'crm'), split_axis=0, concat_axis=0, t...  51.9 us
    all_to_all x1, starting transfers between devices, shards(): lax.all_to_all(heats, ('gcm', 'crm'), split_axis=0, concat_axis=0, tiled=...  36.2 us
    dot_general x16, matrix products, summarize(): heat = jnp.einsum('b,sbc->sc', mass, final - initial, precision=HIGH)  23.2 us
    ppermute x6, starting transfers between devices, with_halo(): lax.ppermute(lax.slice_in_dim(block, 0, width, axis=dim), axis, backward)  21 us
    dot_general x7, matrix products, crm_substep(): jnp.einsum('kq,sqc->skc', collision, pairs.astype(jnp.bfloat16), preferre...  19.1 us
    gather x3, local copies, waits for them, and re-layouts, pack_rows(): taken = jnp.take(values, pick, axis=0)  18.8 us
    convert_element_type x7, other arithmetic, crm_substep(): pairs.astype(jnp.bfloat16)  16.6 us
  transfers between devices with their start and end apart: 17, of which 10 were waited for; matrix products, arithmetic and copies ran while one was open for 14% of the time, Pallas kernels for 0%

commit v1 on v0

v1 whole, which is shorter than its diff:
```python
import functools

import jax
import jax.numpy as jnp
import ml_dtypes
import numpy as np
from jax import lax
from jax.experimental import pallas as pl
from jax.experimental.pallas import tpu as pltpu
from jax.sharding import PartitionSpec as P

BF = jnp.bfloat16
F32 = jnp.float32
MESH = pl.DeviceIdType.MESH
HIGH = lax.Precision.HIGHEST
VMEM = pl.BlockSpec(memory_space=pltpu.VMEM)
SMEM = pl.BlockSpec(memory_space=pltpu.SMEM)

NG = 8
NC = 16
LEV = 72
BINS = 33
CLEV = 16
COLS = 128
PTS = LEV * 8
PAIRS = 576
DT_DYN = 0.04
DT_CRM = 0.05
DT_PHYS = 0.5
BATCH = 4


def gll_tables():
    inv_root = 1.0 / np.sqrt(5.0)
    gll_nodes = np.array([-1.0, -inv_root, inv_root, 1.0])
    weights = np.array([1.0, 5.0, 5.0, 1.0]) / 6.0
    legendre = (5.0 * gll_nodes**3 - 3.0 * gll_nodes) / 2.0
    derivative = np.zeros((4, 4))
    for i in range(4):
        for j in range(4):
            if i != j:
                derivative[i, j] = legendre[i] / (legendre[j] * (gll_nodes[i] - gll_nodes[j]))
    derivative[0, 0] = -3.0
    derivative[3, 3] = 3.0
    return (2.0 * derivative, weights)


def level_tables(levels, crm_levels):
    spacing = levels / crm_levels
    centres = (np.arange(crm_levels) + 0.5) * spacing - 0.5
    hats = np.maximum(0.0, 1.0 - np.abs(np.arange(levels)[None, :] - centres[:, None]) / spacing)
    down_map = hats / hats.sum(axis=1, keepdims=True)
    up_map = hats.T / hats.T.sum(axis=1, keepdims=True)
    return (down_map, up_map)


def stencil_table():
    derivative, _ = gll_tables()
    out = np.zeros((14, 8, 128), np.float32)
    for s in range(-3, 4):
        for i in range(4):
            if 0 <= i + s < 4:
                out[s + 3, i::4, :] = -derivative[i, i + s]
                out[s + 10, :, i::4] = -derivative[i, i + s]
    return out


def forcing_tables():
    _, weights = gll_tables()
    down_map, _ = level_tables(LEV, CLEV)
    rows = np.zeros((2, CLEV, LEV, 8))
    for r in range(8):
        rows[r // 4, :, :, r] = down_map * weights[r % 4] / 2.0 * 0.5
    cols = np.zeros((64, 256))
    for c in range(256):
        cols[c // 4, c] = weights[c % 4] / 2.0
    return rows.reshape(32, PTS).astype(np.float32), cols.astype(np.float32)


def spread_cells():
    out = np.zeros((CLEV, 256), np.float32)
    for c in range(256):
        out[c // 16, c] = 1.0
    return out.astype(ml_dtypes.bfloat16)


def group_matrix():
    out = np.zeros((256, 128), np.float32)
    for c in range(256):
        out[c, c // 16] = 1.0 / 16.0
    return out.astype(ml_dtypes.bfloat16)


def heating_table():
    _, up_map = level_tables(LEV, CLEV)
    half = (DT_PHYS * up_map).astype(np.float32)
    first = half.astype(ml_dtypes.bfloat16)
    second = (half - first.astype(np.float32)).astype(ml_dtypes.bfloat16)
    out = np.zeros((LEV, 8, 2, 2, CLEV), ml_dtypes.bfloat16)
    for r in range(8):
        out[:, r, 0, r // 4, :] = first
        out[:, r, 1, r // 4, :] = second
    return out.reshape(PTS, 64)


def spread_columns():
    out = np.zeros((64, 256), np.float32)
    for c in range(256):
        out[c // 4, c] = 1.0
    return out.astype(ml_dtypes.bfloat16)


def slot_table():
    out = np.zeros((2, 128, 256), np.float32)
    for d in range(128):
        for r in range(2):
            out[r, d, 2 * d + r] = 1.0
    return out.reshape(256, 256).astype(ml_dtypes.bfloat16)


def pair_list():
    out = []
    for d in range(16):
        for i in range(32):
            out.append((i, (i + d) % 32))
    for i in range(16):
        out.append((i, i + 16))
    for i in range(32):
        out.append((i, 32))
    out.append((32, 32))
    return out


def pair_selector():
    out = np.zeros((BINS * BINS, PAIRS), np.float32)
    for q, (i, j) in enumerate(pair_list()):
        out[i * BINS + j, q] = 1.0
        out[j * BINS + i, q] = 1.0
    return out.astype(ml_dtypes.bfloat16)


def split3(x):
    hi = x.astype(BF)
    rest = x - hi.astype(F32)
    mid = rest.astype(BF)
    return hi, mid, (rest - mid.astype(F32)).astype(BF)


def dot_exact(onehot, x):
    acc = None
    for part in split3(x):
        y = jnp.dot(onehot, part, preferred_element_type=F32)
        acc = y if acc is None else acc + y
    return acc


def tendency(q, wind_x, wind_y, table):
    grad_x = table[3][None] * q
    grad_y = table[10][None] * q
    for s in (-3, -2, -1, 1, 2, 3):
        grad_x = grad_x + table[s + 3][None] * pltpu.roll(q, (-s) % 8, 1)
        grad_y = grad_y + table[s + 10][None] * pltpu.roll(q, (-s) % 128, 2)
    return wind_x * grad_x + wind_y * grad_y


def neighbours():
    g = lax.axis_index("gcm")
    c = lax.axis_index("crm")
    up, down = lax.rem(g + NG - 1, NG), lax.rem(g + 1, NG)
    left, right = lax.rem(c + NC - 1, NC), lax.rem(c + 1, NC)
    return g, c, up, down, left, right


def pack_edges(field, packs, rows):
    lane = lax.broadcasted_iota(jnp.int32, (8, 128), 1)

    def one(i, carry):
        low, high = carry
        low, high = pltpu.roll(low, 120, 1), pltpu.roll(high, 120, 1)
        for k in range(8):
            at = pl.multiple_of(i * 64, 64) + 8 * k
            first, last = field[pl.ds(at, 8), :], field[pl.ds(PTS + at, 8), :]
            both = pltpu.roll(jnp.where(lane == 0, first, last), k + 1, 1)
            high = jnp.where(lane == k, both, high)
            low = jnp.where(lane == k + 1, both, low)
        return low, high

    zero = jnp.zeros((8, 128), F32)
    low, high = lax.fori_loop(0, 9, one, (zero, zero))
    packs[0] = pltpu.roll(low, 63, 1)
    packs[1] = pltpu.roll(high, 64, 1)
    for half in range(2):
        rows[0, half * LEV : (half + 1) * LEV, :] = field[pl.ds(half * PTS, LEV, stride=8), :]
        rows[1, half * LEV : (half + 1) * LEV, :] = field[pl.ds(half * PTS + 7, LEV, stride=8), :]


def halo_copies(packs, rows, got_packs, got_rows, send, recv):
    g, c, up, down, left, right = neighbours()
    plan = [
        (rows.at[1], got_rows.at[0], (down, c)),
        (rows.at[0], got_rows.at[1], (up, c)),
        (packs.at[1], got_packs.at[0], (g, right)),
        (packs.at[1], got_packs.at[1], (down, right)),
        (packs.at[1], got_packs.at[2], (up, right)),
        (packs.at[0], got_packs.at[3], (g, left)),
        (packs.at[0], got_packs.at[4], (down, left)),
        (packs.at[0], got_packs.at[5], (up, left)),
    ]
    return [
        pltpu.make_async_remote_copy(
            src_ref=src,
            dst_ref=dst,
            send_sem=send.at[n],
            recv_sem=recv.at[n],
            device_id=to,
            device_id_type=MESH,
        )
        for n, (src, dst, to) in enumerate(plan)
    ]


def assemble_loop(field, got_packs, got_rows, use):
    row = lax.broadcasted_iota(jnp.int32, (8, 128), 0)
    lane = lax.broadcasted_iota(jnp.int32, (8, 128), 1)

    def row_mean(x, above, below):
        up = jnp.where(row == 0, pltpu.roll(above, 1, 0), pltpu.roll(x, 1, 0))
        down = jnp.where(row == 7, pltpu.roll(below, 7, 0), pltpu.roll(x, 7, 0))
        other = jnp.where(row % 4 == 3, down, jnp.where(row % 4 == 0, up, x))
        return 0.5 * (x + other)

    left_halo = row_mean(got_packs[0], got_packs[1], got_packs[2])
    right_halo = row_mean(got_packs[3], got_packs[4], got_packs[5])
    edge_row = ((row == 0) | (row == 7))[None]
    upper = (row < 4)[None]
    is3, is4 = (row == 3)[None], (row == 4)[None]
    lane3, lane0 = (lane % 4 == 3)[None], (lane % 4 == 0)[None]
    first, last = (lane == 0)[None], (lane == 127)[None]

    def one(i, carry):
        left_c, right_c = carry
        means = []
        for half in range(2):
            at = pl.multiple_of(half * PTS + i * 64, 64)
            x = field[pl.ds(at, 64), :].reshape(8, 8, 128)
            lev = pl.multiple_of(half * LEV + i * 8, 8)
            above = jnp.broadcast_to(got_rows[0, pl.ds(lev, 8), :][:, None, :], (8, 8, 128))
            below = jnp.broadcast_to(got_rows[1, pl.ds(lev, 8), :][:, None, :], (8, 8, 128))
            other = jnp.where(is3, pltpu.roll(x, 7, 1), jnp.where(is4, pltpu.roll(x, 1, 1), x))
            other = jnp.where(edge_row, jnp.where(upper, above, below), other)
            means.append(0.5 * (x + other))
        lefts = [pltpu.roll(m, 1, 2) for m in means]
        rights = [pltpu.roll(m, 127, 2) for m in means]
        halo_l = jnp.stack([pltpu.roll(left_c, (128 - k) % 128, 1) if k else left_c for k in range(8)])
        halo_r = jnp.stack([pltpu.roll(right_c, 127 - k, 1) for k in range(8)])
        near_l = [jnp.where(first, halo_l, lefts[0]), jnp.where(first, lefts[0], lefts[1])]
        near_r = [jnp.where(last, rights[1], rights[0]), jnp.where(last, halo_r, rights[1])]
        for half in range(2):
            m = means[half]
            other = jnp.where(lane3, near_r[half], jnp.where(lane0, near_l[half], m))
            use(i, half, 0.5 * (m + other))
        return pltpu.roll(left_c, 120, 1), pltpu.roll(right_c, 120, 1)

    lax.fori_loop(0, 9, one, (left_halo, right_halo))


def chunk_of(ref, i, half):
    return ref[pl.ds(i * 8, 8), :, half * 128 : (half + 1) * 128]


def dynamics_kernel(
    tracer, wind_x, wind_y, counts, collision, table, selector, row_map, col_map, cells,
    state, cell_forcing, pair_coef, order, rank,
    field, total, packs, rows, got_packs, got_rows, send, recv,
):
    g, c, up, down, left, right = neighbours()
    barrier = pltpu.get_barrier_semaphore()
    around = [(up, c), (down, c)]
    around += [(r, s) for s in (left, right) for r in (g, up, down)]
    for to in around:
        pl.semaphore_signal(barrier, inc=1, device_id=to, device_id_type=MESH)

    def first(i, _):
        for half in range(2):
            t = tendency(
                chunk_of(tracer, i, half), chunk_of(wind_x, i, half), chunk_of(wind_y, i, half), table
            )
            field[pl.ds(pl.multiple_of(half * PTS + i * 64, 64), 64), :] = t.reshape(64, 128)
        return 0

    lax.fori_loop(0, 9, first, 0)
    pack_edges(field, packs.at[0], rows.at[0])
    pl.semaphore_wait(barrier, 8)
    copies = halo_copies(packs.at[0], rows.at[0], got_packs.at[0], got_rows.at[0], send.at[0], recv.at[0])
    for copy in copies:
        copy.start()

    pair_coef[0:33, :] = jnp.dot(
        collision[...], selector[...], preferred_element_type=F32
    ).astype(BF)
    pair_coef[33:48, :] = jnp.zeros((15, PAIRS), BF)
    across = jnp.broadcast_to(counts[...], (COLS, COLS)).astype(F32)
    i0 = lax.broadcasted_iota(jnp.int32, (COLS, COLS), 0)
    i1 = lax.broadcasted_iota(jnp.int32, (COLS, COLS), 1)
    along = jnp.sum(jnp.where(i0 == i1, across, 0.0), axis=1, keepdims=True)
    before = (across > along) | ((across == along) & (i1 < i0))
    place = jnp.sum(jnp.where(before, 1.0, 0.0), axis=1, keepdims=True)
    place = jnp.broadcast_to(place, (COLS, COLS)).astype(jnp.int32)
    rank[...] = place
    listed = jnp.sum(jnp.where(place == i1, i0.astype(F32), 0.0), axis=0, keepdims=True)
    order[...] = listed.astype(jnp.int32)

    for copy in copies:
        copy.wait()

    def second(i, half, mean):
        at = pl.multiple_of(half * PTS + i * 64, 64)
        moved = chunk_of(tracer, i, half) + DT_DYN * mean
        state[pl.ds(i * 8, 8), :, half * 128 : (half + 1) * 128] = moved
        total[pl.ds(at, 64), :] = mean.reshape(64, 128)
        t = tendency(moved, chunk_of(wind_x, i, half), chunk_of(wind_y, i, half), table)
        field[pl.ds(at, 64), :] = t.reshape(64, 128)

    assemble_loop(field, got_packs.at[0], got_rows.at[0], second)
    pack_edges(field, packs.at[1], rows.at[1])
    copies = halo_copies(packs.at[1], rows.at[1], got_packs.at[1], got_rows.at[1], send.at[1], recv.at[1])
    for copy in copies:
        copy.start()
    for copy in copies:
        copy.wait()

    def third(i, half, mean):
        at = pl.multiple_of(half * PTS + i * 64, 64)
        state[pl.ds(i * 8, 8), :, half * 128 : (half + 1) * 128] = (
            chunk_of(state, i, half) + DT_DYN * mean
        )
        total[pl.ds(at, 64), :] = total[pl.ds(at, 64), :] + mean.reshape(64, 128)

    assemble_loop(field, got_packs.at[1], got_rows.at[1], third)
    parts = [
        jnp.dot(row_map[...], total[half * PTS : (half + 1) * PTS, :], precision=HIGH, preferred_element_type=F32)
        for half in range(2)
    ]
    by_row = jnp.concatenate(parts, axis=1)
    for e in range(2):
        forcing = lax.dot_general(
            col_map[...], by_row[16 * e : 16 * (e + 1)], (((1,), (1,)), ((), ())),
            precision=HIGH, preferred_element_type=F32,
        ).astype(BF)
        cell_forcing[64 * e : 64 * (e + 1), :] = DT_CRM * jnp.dot(
            forcing, cells[...], preferred_element_type=F32
        )


def dynamics(tracer, wind_x, wind_y, counts_row, collision):
    row_map, col_map = forcing_tables()
    shape = tracer.shape
    return pl.pallas_call(
        dynamics_kernel,
        out_shape=(
            jax.ShapeDtypeStruct(shape, F32),
            jax.ShapeDtypeStruct((COLS, 256), F32),
            jax.ShapeDtypeStruct((48, PAIRS), BF),
            jax.ShapeDtypeStruct((1, COLS), jnp.int32),
            jax.ShapeDtypeStruct((COLS, COLS), jnp.int32),
        ),
        in_specs=[VMEM] * 10,
        out_specs=(VMEM,) * 5,
        scratch_shapes=[
            pltpu.VMEM((2 * PTS, 128), F32),
            pltpu.VMEM((2 * PTS, 128), F32),
            pltpu.VMEM((2, 2, 8, 128), F32),
            pltpu.VMEM((2, 2, 2 * LEV, 128), F32),
            pltpu.VMEM((2, 6, 8, 128), F32),
            pltpu.VMEM((2, 2, 2 * LEV, 128), F32),
            pltpu.SemaphoreType.DMA((2, 8)),
            pltpu.SemaphoreType.DMA((2, 8)),
        ],
        compiler_params=pltpu.CompilerParams(
            collective_id=0, has_side_effects=True, vmem_limit_bytes=40 << 20
        ),
        name="dynamics",
    )(
        tracer, wind_x, wind_y, counts_row, collision,
        jnp.asarray(stencil_table()), jnp.asarray(pair_selector()),
        jnp.asarray(row_map), jnp.asarray(col_map), jnp.asarray(spread_cells()),
    )


def micro_kernel(
    order, counts, drops, cell_forcing, pair_coef, growth, group, rank,
    drops_next, heat_out, echo_out,
    cloud, doubled, grow, heat_rows, echo_rows,
):
    mass = (lax.broadcasted_iota(jnp.int32, (40, 128), 0).astype(F32) + 1.0) / BINS
    srow = lax.broadcasted_iota(jnp.int32, (8, 128), 0)

    def substep(s, p):
        for b in range(BATCH):
            active = s < counts[order[0, p * BATCH + b]]
            blocks, grown, olds = [], [], []
            for half in range(2):
                old = cloud[b, half]
                now = old + grow[b, half]
                doubled[b, half, 0:32, :] = now[0:32]
                doubled[b, half, 32:48, :] = now[0:16]
                near, far = [], []
                for d in range(8):
                    shifted = doubled[b, half, d : d + 40, :]
                    near.append((now[0:32] * shifted[0:32]).astype(BF))
                    far.append((now[0:32] * shifted[8:40]).astype(BF))
                last = jnp.broadcast_to(now[32:33], (32, 128))
                rest = [
                    (now[0:16] * now[16:32]).astype(BF),
                    (now[0:32] * last).astype(BF),
                    (last[0:16] * last[0:16]).astype(BF),
                ]
                blocks.append(jnp.concatenate(near + far + rest, axis=0))
                grown.append(now)
                olds.append(old)
            change = jnp.dot(
                pair_coef[...], jnp.concatenate(blocks, axis=1), preferred_element_type=F32
            )
            for half in range(2):
                moved = grown[half] + DT_CRM * change[0:40, half * 128 : (half + 1) * 128]
                cloud[b, half] = jnp.where(active, moved, olds[half])
        return p

    def batch(p, _):
        for b in range(BATCH):
            col = order[0, p * BATCH + b]
            forced = cell_forcing[pl.ds(col, 1), :]
            for half in range(2):
                at = slice(half * 128, (half + 1) * 128)
                cloud[b, half, 0:32, :] = drops[col, 0:32, at].astype(F32)
                cloud[b, half, 32:40, :] = jnp.broadcast_to(drops[col, 32:33, at].astype(F32), (8, 128))
                grow[b, half] = forced[:, at] * growth[...]
        lax.fori_loop(0, counts[order[0, p * BATCH]], substep, p)
        heats = [jnp.zeros((8, 128), F32)] * 2
        echos = [jnp.zeros((8, 128), F32)] * 2
        for b in range(BATCH):
            col = order[0, p * BATCH + b]
            for half in range(2):
                at = slice(half * 128, (half + 1) * 128)
                final = cloud[b, half]
                drops_next[col, 0:32, at] = final[0:32].astype(BF)
                drops_next[col, 32:33, at] = final[32:33].astype(BF)
                gain = (final[0:32] - drops[col, 0:32, at].astype(F32)) * mass[0:32]
                gain_last = (final[32:33] - drops[col, 32:33, at].astype(F32)) * mass[32:33]
                weighed = final * mass
                square = weighed * weighed
                heats[half] = jnp.where(
                    srow == b, jnp.sum(gain, axis=0, keepdims=True) + gain_last, heats[half]
                )
                echos[half] = jnp.where(
                    srow == b, jnp.sum(square[0:32], axis=0, keepdims=True) + square[32:33], echos[half]
                )
        for half in range(2):
            at = slice(half * 128, (half + 1) * 128)
            heat_rows[p, :, at] = heats[half]
            echo_rows[p, :, at] = echos[half]
        return 0

    lax.fori_loop(0, COLS // BATCH, batch, 0)
    total = COLS // BATCH * 8
    q = lax.broadcasted_iota(jnp.int32, (COLS, total), 1)
    pick = ((q // 8 * BATCH + q % 8 == rank[:, 0:1]) & (q % 8 < BATCH)).astype(F32).astype(BF)

    def group_mean(x):
        acc = None
        for part in split3(x):
            y = jnp.dot(part, group[...], preferred_element_type=F32)
            acc = y if acc is None else acc + y
        return acc

    heat = group_mean(heat_rows[...].reshape(total, 256)).astype(BF)
    heat_out[...] = jnp.dot(pick, heat, preferred_element_type=F32).astype(BF)
    echo_out[...] = jnp.log(1.0 + dot_exact(pick, group_mean(echo_rows[...].reshape(total, 256))))


def microphysics(order, counts, drops, cell_forcing, pair_coef, growth, rank):
    return pl.pallas_call(
        micro_kernel,
        out_shape=(
            jax.ShapeDtypeStruct(drops.shape, BF),
            jax.ShapeDtypeStruct((COLS, 128), BF),
            jax.ShapeDtypeStruct((COLS, 128), F32),
        ),
        in_specs=[SMEM, SMEM] + [VMEM] * 6,
        out_specs=(VMEM,) * 3,
        scratch_shapes=[
            pltpu.VMEM((BATCH, 2, 40, 128), F32),
            pltpu.VMEM((BATCH, 2, 48, 128), F32),
            pltpu.VMEM((BATCH, 2, 40, 128), F32),
            pltpu.VMEM((COLS // BATCH, 8, 256), F32),
            pltpu.VMEM((COLS // BATCH, 8, 256), F32),
        ],
        compiler_params=pltpu.CompilerParams(vmem_limit_bytes=40 << 20),
        name="microphysics",
    )(order, counts, drops, cell_forcing, pair_coef, growth, jnp.asarray(group_matrix()), rank)


def coupling_kernel(
    state, heat, echo, owner, heating, spread, slots,
    tracer_next, power,
    field, packs, rows, got_packs, got_rows, sent, first_in, second_out, second_in,
    send, recv, send1, recv1, send2, recv2,
):
    g, c, up, down, left, right = neighbours()
    barrier = pltpu.get_barrier_semaphore()
    peers = [(lax.rem(g + k, NG), c) for k in range(1, NG)]
    peers += [(g, lax.rem(c + k, NC)) for k in range(1, NC)]
    peers += [(r, s) for s in (left, right) for r in (up, down)]
    for to in peers:
        pl.semaphore_signal(barrier, inc=1, device_id=to, device_id_type=MESH)

    warm = []
    for e in range(2):
        turned = heat[64 * e : 64 * (e + 1), :].astype(F32).T.astype(BF)[0:16]
        warm.append(jnp.dot(turned, spread[...], preferred_element_type=F32).astype(BF))
    warm = jnp.concatenate(warm + warm, axis=0)
    for half in range(2):
        at = slice(half * 128, (half + 1) * 128)
        back = jnp.dot(heating[...], warm[:, at], preferred_element_type=F32)
        field[half * PTS : (half + 1) * PTS, :] = back + state[:, :, at].reshape(PTS, 128)
    pack_edges(field, packs, rows)
    pl.semaphore_wait(barrier, len(peers))
    copies = halo_copies(packs, rows, got_packs, got_rows, send, recv)
    for copy in copies:
        copy.start()

    across = jnp.broadcast_to(owner[...], (COLS, COLS))
    i0 = lax.broadcasted_iota(jnp.int32, (COLS, COLS), 0)
    i1 = lax.broadcasted_iota(jnp.int32, (COLS, COLS), 1)
    along = jnp.sum(jnp.where(i0 == i1, across.astype(F32), 0.0), axis=1, keepdims=True)
    earlier = (along == across.astype(F32)) & (i0 < i1)
    turn = jnp.sum(jnp.where(earlier, 1.0, 0.0), axis=0, keepdims=True)
    key = across % NC * NG + across // NC
    onehot = jnp.concatenate(
        [jnp.where((key == i0) & (turn == float(r)), 1.0, 0.0) for r in range(2)], axis=1
    ).astype(BF)
    sums = echo[...]
    sums = jnp.concatenate([sums, pltpu.roll(sums, 16, 1)], axis=0)
    sent[...] = dot_exact(onehot, sums).reshape(NC, NG, 128)
    first = []
    for k in range(1, NC):
        to = lax.rem(c + k, NC)
        copy = pltpu.make_async_remote_copy(
            src_ref=sent.at[to],
            dst_ref=first_in.at[c],
            send_sem=send1.at[k],
            recv_sem=recv1.at[c],
            device_id=(g, to),
            device_id_type=MESH,
        )
        copy.start()
        first.append(copy)
    first_in[c] = sent[c]

    for copy in copies:
        copy.wait()

    def last(i, half, mean):
        tracer_next[pl.ds(i * 8, 8), :, half * 128 : (half + 1) * 128] = mean

    assemble_loop(field, got_packs, got_rows, last)

    for k, copy in enumerate(first, 1):
        copy.wait_send()
        source = lax.rem(c + k, NC)
        pltpu.make_async_remote_copy(
            src_ref=sent.at[source],
            dst_ref=first_in.at[source],
            send_sem=send1.at[k],
            recv_sem=recv1.at[source],
            device_id=(g, source),
            device_id_type=MESH,
        ).wait_recv()
    every = first_in[...]
    for to in range(NG):
        second_out[to] = every[:, to, :]
    second = []
    for k in range(1, NG):
        to = lax.rem(g + k, NG)
        copy = pltpu.make_async_remote_copy(
            src_ref=second_out.at[to],
            dst_ref=second_in.at[g],
            send_sem=send2.at[k],
            recv_sem=recv2.at[g],
            device_id=(to, c),
            device_id_type=MESH,
        )
        copy.start()
        second.append(copy)
    second_in[g] = second_out[g]
    for k, copy in enumerate(second, 1):
        copy.wait_send()
        source = lax.rem(g + k, NG)
        pltpu.make_async_remote_copy(
            src_ref=second_out.at[source],
            dst_ref=second_in.at[source],
            send_sem=send2.at[k],
            recv_sem=recv2.at[source],
            device_id=(source, c),
            device_id_type=MESH,
        ).wait_recv()
    turned = second_in[...].reshape(COLS, 128).T
    turned = jnp.concatenate([turned[0:16], turned[16:32]], axis=1)
    acc = None
    for part in split3(turned):
        y = jnp.dot(part, slots[...], preferred_element_type=F32)
        acc = y if acc is None else acc + y
    power[...] = acc


def coupling(state, heat, echo, owner_row):
    return pl.pallas_call(
        coupling_kernel,
        out_shape=(
            jax.ShapeDtypeStruct(state.shape, F32),
            jax.ShapeDtypeStruct((CLEV, 256), F32),
        ),
        in_specs=[VMEM] * 7,
        out_specs=(VMEM,) * 2,
        scratch_shapes=[
            pltpu.VMEM((2 * PTS, 128), F32),
            pltpu.VMEM((2, 8, 128), F32),
            pltpu.VMEM((2, 2 * LEV, 128), F32),
            pltpu.VMEM((6, 8, 128), F32),
            pltpu.VMEM((2, 2 * LEV, 128), F32),
            pltpu.VMEM((NC, NG, 128), F32),
            pltpu.VMEM((NC, NG, 128), F32),
            pltpu.VMEM((NG, NC, 128), F32),
            pltpu.VMEM((NG, NC, 128), F32),
            pltpu.SemaphoreType.DMA((8,)),
            pltpu.SemaphoreType.DMA((8,)),
            pltpu.SemaphoreType.DMA((NC,)),
            pltpu.SemaphoreType.DMA((NC,)),
            pltpu.SemaphoreType.DMA((NG,)),
            pltpu.SemaphoreType.DMA((NG,)),
        ],
        compiler_params=pltpu.CompilerParams(
            collective_id=1, has_side_effects=True, vmem_limit_bytes=40 << 20
        ),
        name="coupling",
    )(
        state, heat, echo, owner_row,
        jnp.asarray(heating_table()), jnp.asarray(spread_columns()), jnp.asarray(slot_table()),
    )


def shards(tracer, wind_x, wind_y, drops, owner, counts, collision, growth):
    state, cell_forcing, pair_coef, order, rank = dynamics(
        tracer, wind_x, wind_y, counts.reshape(1, COLS), collision
    )
    column = jnp.broadcast_to(jnp.pad(growth, (0, 7))[:, None], (40, 128))
    drops_next, heat, echo = microphysics(
        order, counts, drops, cell_forcing, pair_coef, column, rank
    )
    tracer_next, power = coupling(state, heat, echo, owner.reshape(1, COLS))
    return (tracer_next, drops_next, power)


def solution(mesh):
    return jax.shard_map(
        shards,
        mesh=mesh,
        in_specs=(
            P(None, "gcm", "crm"),
            P(None, "gcm", "crm"),
            P(None, "gcm", "crm"),
            P(("gcm", "crm"), None, None),
            P(("gcm", "crm"), None),
            P(("gcm", "crm")),
            P(),
            P(),
        ),
        out_specs=(P(None, "gcm", "crm"), P(("gcm", "crm"), None, None), P(None, ("gcm", "crm"))),
        check_vma=False,
    )
```

time: 496 us -> 99.7 us (0.20); the launches traced: 487 us -> 98.1 us
  waiting for transfers between devices: 124 us -> 0 us
  other arithmetic: 115 us -> 0 us
  starting transfers between devices: 88.4 us -> 0 us
  Pallas kernels: 0 us -> 82.7 us
  local copies, waits for them, and re-layouts: 80.1 us -> 14.6 us
  matrix products: 60.8 us -> 0 us
  loops' own time: 17.8 us -> 0 us
    pallas_call x0 -> x3, Pallas kernels: none -> 82.7 us  [the longest x1 48.4 us: coupling(): pl.pallas_call(coupling_kernel, out_shape=(jax.ShapeDtypeStruct(state.sha...]
    all_to_all x5 -> x0, starting transfers between devices: 66.5 us -> none  [the longest x1 36.2 us: shards(): lax.all_to_all(heats, ('gcm', 'crm'), split_axis=0, concat_axis=0, tiled=...]
    ppermute x12 -> x0, waiting for transfers between devices: 66.4 us -> none  [the longest x6 52 us: with_halo(): lax.ppermute(lax.slice_in_dim(block, 0, width, axis=dim), axis, backward)]
    dot_general x45 -> x0, matrix products: 60.8 us -> none  [the longest x16 23.2 us: summarize(): heat = jnp.einsum('b,sbc->sc', mass, final - initial, precision=HIGH)]
    all_to_all x5 -> x0, waiting for transfers between devices: 57.1 us -> none  [the longest x1 51.9 us: shards(): lax.all_to_all(send_drops, ('gcm', 'crm'), split_axis=0, concat_axis=0, t...]
    gather x11 -> x0, local copies, waits for them, and re-layouts: 40.2 us -> none  [the longest x3 18.8 us: pack_rows(): taken = jnp.take(values, pick, axis=0)]
    convert_element_type x42 -> x0, other arithmetic: 34.5 us -> none  [the longest x7 16.6 us: crm_substep(): pairs.astype(jnp.bfloat16)]
    ppermute x12 -> x0, starting transfers between devices: 21.9 us -> none  [the longest x6 21 us: with_halo(): lax.ppermute(lax.slice_in_dim(block, 0, width, axis=dim), axis, backward)]
  transfers between devices with their start and end apart: 17 -> 0, of which waited for: 10 -> 0; matrix products, arithmetic and copies ran while one was open for 14% -> 0% of each run, Pallas kernels for 0% -> 0%
where the time goes in v1:
time: 99.7 us; the launch traced here: 98.1 us
  Pallas kernels  82.7 us (83%)
  local copies, waits for them, and re-layouts  14.6 us (15%)
    pallas_call x1, Pallas kernels, coupling(): pl.pallas_call(coupling_kernel, out_shape=(jax.ShapeDtypeStruct(state.sha...  48.4 us
    pallas_call x1, Pallas kernels, dynamics(): pl.pallas_call(dynamics_kernel, out_shape=(jax.ShapeDtypeStruct(shape, F3...  24.1 us
    unnamed x38, local copies, waits for them, and re-layouts  13.9 us
    pallas_call x1, Pallas kernels, microphysics(): pl.pallas_call(micro_kernel, out_shape=(jax.ShapeDtypeStruct(drops.shape,...  10.2 us

profile of v1, /device:TPU:0, one launch (start us, length us, event | category | flops | bytes accessed | tf_op | source)
XLA Modules:
  0.0 98.1 jit_solution(12865360180547135690)
XLA Ops:
  0.6 0.7 pad.4
  1.3 0.1 broadcast_in_dim.2.growth
  1.4 1.3 %copy-done = bf16[1089,576]{1,0:T(8,128)(2,1)S(1)} copy-done((bf16[1089,576]{1,0:T(8,128)(2,1)S(1)}, bf16[1089,576]{1,0:T(8,128)(2,1)}, u32[]{:S(2)}) %copy-start) | copy-done | bytes 1254552
  2.7 1.1 %copy-done.1 = f32[72,8,256]{2,1,0:T(8,128)S(1)} copy-done((f32[72,8,256]{2,1,0:T(8,128)S(1)}, f32[72,8,256]{2,1,0:T(8,128)}, u32[]{:S(2)}) %copy-start.1) | copy-done | bytes 589848
  3.8 1.1 %copy-done.2 = f32[72,8,256]{2,1,0:T(8,128)S(1)} copy-done((f32[72,8,256]{2,1,0:T(8,128)S(1)}, f32[72,8,256]{2,1,0:T(8,128)}, u32[]{:S(2)}) %copy-start.2) | copy-done | bytes 589848
  4.8 1.1 %copy-done.3 = f32[72,8,256]{2,1,0:T(8,128)S(1)} copy-done((f32[72,8,256]{2,1,0:T(8,128)S(1)}, f32[72,8,256]{2,1,0:T(8,128)}, u32[]{:S(2)}) %copy-start.3) | copy-done | bytes 589848
  5.9 0.9 copy-done.6
  6.8 0.9 copy-done.7
  7.7 0.8 copy-done.9
  8.5 0.8 copy-done.10
  9.3 0.7 copy-done.12
  10.0 0.7 copy-done.13
  10.7 24.1 %dynamics.1 = (f32[72,8,256]{2,1,0:T(8,128)S(1)}, f32[128,256]{1,0:T(8,128)S(1)}, bf16[48,576]{1,0:T(8,128)(2,1)S(1)}, s32[1,128]{1,0:T(1,128)S(1)}, s32[128,128]{1,0:T(8,128)S(1)}) custom-call(f32[72,8,256]{2,1,0:T(8,128)S(1)} %copy-done.1, f32[72,8,256]{2,1,0:T(8,128)S(1)} %copy-done.2, f32[72,8,256]{2,1,0:T(8,128)S(1)} %copy-done.3, ...), custom_call_target="tpu_custom_call" | custom-call | tf_op jit(solution)/shard_map/dynamics/pallas_call | solution.py:358
  34.9 0.0 copy-start.8
  34.9 1.3 %copy.20.drops = bf16[128,33,256]{2,1,0:T(8,128)(2,1)S(1)} copy(bf16[128,33,256]{2,0,1:T(8,128)(2,1)S(1)} %copy-done.16) | data formatting | bytes 4325376 | tf_op args[3]
  36.2 0.0 copy-start.4
  36.2 0.0 copy-start.5
  36.2 0.0 copy-start.11
  36.2 0.0 copy-start.15
  36.2 10.2 %microphysics.1 = (bf16[128,33,256]{2,1,0:T(8,128)(2,1)S(1)}, bf16[128,128]{1,0:T(8,128)(2,1)S(1)}, f32[128,128]{1,0:T(8,128)S(1)}) custom-call(s32[1,128]{1,0:T(1,128)S(1)} %get-tuple-element.14.order, s32[128]{0:T(128)S(1)} %copy-done.14, bf16[128,33,256]{2,1,0:T(8,128)(2,1)S(1)} %copy.20.drops, f32[128,256]{1,0:T(8,128)S(1)} %get-tuple-element.15.cell_forcing, ...), custom_call_target="tpu_custom_call" | custom-call | tf_op jit(solution)/shard_map/microphysics/pallas_call | solution.py:482
  46.5 48.4 %coupling.1 = (f32[72,8,256]{2,1,0:T(8,128)S(1)}, f32[16,256]{1,0:T(8,128)S(1)}) custom-call(f32[72,8,256]{2,1,0:T(8,128)S(1)} %get-tuple-element.13.state, bf16[128,128]{1,0:T(8,128)(2,1)S(1)} %get-tuple-element.18.heat, f32[128,128]{1,0:T(8,128)S(1)} %get-tuple-element.19.echo, s32[1,128]{1,0:T(1,128)S(1)} %bitcast.3, bf16[576,64]{1,0:T(8,128)(2,1)S(1)} %copy-done.4, ...), custom_call_target="tpu_custom_call" | custom-call | tf_op jit(solution)/shard_map/coupling/pallas_call | solution.py:617
  94.9 1.8 %copy.21 = bf16[128,33,256]{2,0,1:T(8,128)(2,1)} copy(bf16[128,33,256]{2,1,0:T(8,128)(2,1)S(1)} %get-tuple-element.24) | data formatting | bytes 4325376
  96.7 0.8 copy.24
  97.5 0.6 copy.25
  (19 shorter events, 0.0 us)
Async XLA Ops:
  1.4 1.4 %copy-start = (bf16[1089,576]{1,0:T(8,128)(2,1)S(1)}, bf16[1089,576]{1,0:T(8,128)(2,1)}, u32[]{:S(2)}) copy-start(bf16[1089,576]{1,0:T(8,128)(2,1)} %constant.22.clone.selector) | copy-start | bytes 3763588
  2.7 1.1 %copy-start.1 = (f32[72,8,256]{2,1,0:T(8,128)S(1)}, f32[72,8,256]{2,1,0:T(8,128)}, u32[]{:S(2)}) copy-start(f32[72,8,256]{2,1,0:T(8,128)} %tracer.1) | copy-start | bytes 1769476
  3.8 1.1 %copy-start.2 = (f32[72,8,256]{2,1,0:T(8,128)S(1)}, f32[72,8,256]{2,1,0:T(8,128)}, u32[]{:S(2)}) copy-start(f32[72,8,256]{2,1,0:T(8,128)} %wind_x.1) | copy-start | bytes 1769476
  4.8 1.1 %copy-start.3 = (f32[72,8,256]{2,1,0:T(8,128)S(1)}, f32[72,8,256]{2,1,0:T(8,128)}, u32[]{:S(2)}) copy-start(f32[72,8,256]{2,1,0:T(8,128)} %wind_y.1) | copy-start | bytes 1769476
  5.9 0.9 copy-start.6
  6.8 0.9 copy-start.7
  7.7 0.8 copy-start.9
  8.5 0.8 copy-start.10
  9.3 0.7 copy-start.12
  10.0 0.7 copy-start.13
  10.7 24.1 %copy-start.16 = (bf16[128,33,256]{2,0,1:T(8,128)(2,1)S(1)}, bf16[128,33,256]{2,0,1:T(8,128)(2,1)}, u32[]{:S(2)}) copy-start(bf16[128,33,256]{2,0,1:T(8,128)(2,1)} %param.20) | copy-start | bytes 6488068
  34.9 1.3 %copy-start.8 = (bf16[256,128]{1,0:T(8,128)(2,1)S(1)}, bf16[256,128]{1,0:T(8,128)(2,1)}, u32[]{:S(2)}) copy-start(bf16[256,128]{1,0:T(8,128)(2,1)} %constant.26.clone.group) | copy-start | bytes 196612
  34.9 1.3 %copy-start.14 = (s32[128]{0:T(128)S(1)}, s32[128]{0:T(128)}, u32[]{:S(2)}) copy-start(s32[128]{0:T(128)} %counts.1) | copy-start | bytes 1540
  36.2 10.3 %copy-start.4 = (bf16[576,64]{1,0:T(8,128)(2,1)S(1)}, bf16[576,64]{1,0:T(8,128)(2,1)}, u32[]{:S(2)}) copy-start(bf16[576,64]{1,0:T(8,128)(2,1)} %constant.27.clone.heating) | copy-start | bytes 221188
  36.2 10.3 %copy-start.5 = (bf16[256,256]{1,0:T(8,128)(2,1)S(1)}, bf16[256,256]{1,0:T(8,128)(2,1)}, u32[]{:S(2)}) copy-start(bf16[256,256]{1,0:T(8,128)(2,1)} %constant.29.clone.slots) | copy-start | bytes 393220
  36.2 10.3 %copy-start.11 = (bf16[64,256]{1,0:T(8,128)(2,1)S(1)}, bf16[64,256]{1,0:T(8,128)(2,1)}, u32[]{:S(2)}) copy-start(bf16[64,256]{1,0:T(8,128)(2,1)} %constant.28.clone.spread) | copy-start | bytes 98308
  36.2 10.3 %copy-start.15 = (s32[128,1]{0,1:T(1,128)S(1)}, s32[128,1]{0,1:T(1,128)}, u32[]{:S(2)}) copy-start(s32[128,1]{0,1:T(1,128)} %param.21) | copy-start | bytes 1540

commit v2 on v1

--- a/solution.py
+++ b/solution.py
@@ -15,6 +15,7 @@
 HIGH = lax.Precision.HIGHEST
 VMEM = pl.BlockSpec(memory_space=pltpu.VMEM)
 SMEM = pl.BlockSpec(memory_space=pltpu.SMEM)
+HBM = pl.BlockSpec(memory_space=pltpu.HBM)
 
 NG = 8
 NC = 16
@@ -27,7 +28,8 @@
 DT_DYN = 0.04
 DT_CRM = 0.05
 DT_PHYS = 0.5
-BATCH = 4
+BATCH = 16
+ROWS = 40
 
 
 def gll_tables():
@@ -269,16 +271,30 @@
 
 
 def dynamics_kernel(
-    tracer, wind_x, wind_y, counts, collision, table, selector, row_map, col_map, cells,
-    state, cell_forcing, pair_coef, order, rank,
-    field, total, packs, rows, got_packs, got_rows, send, recv,
+    tracer_h, wind_x_h, wind_y_h, drops_h, counts_h, growth_h, collision_h, table_h, selector_h,
+    row_map_h, col_map_h, cells_h,
+    state, cell_forcing, pair_coef, growth_col, start, counts_out, unsort,
+    tracer, wind_x, wind_y, drops, counts, growth, collision, table, selector, row_map, col_map, cells,
+    loads, field, total, packs, rows, got_packs, got_rows, send, recv,
 ):
     g, c, up, down, left, right = neighbours()
     barrier = pltpu.get_barrier_semaphore()
     around = [(up, c), (down, c)]
     around += [(r, s) for s in (left, right) for r in (g, up, down)]
+    sources = [table_h, tracer_h, wind_x_h, wind_y_h, counts_h, growth_h, collision_h, selector_h, drops_h,
+               row_map_h, col_map_h, cells_h]
+    targets = [table, tracer, wind_x, wind_y, counts, growth, collision, selector, drops,
+               row_map, col_map, cells]
+    fetch = [
+        pltpu.make_async_copy(source, target, loads.at[n])
+        for n, (source, target) in enumerate(zip(sources, targets))
+    ]
+    for copy in fetch:
+        copy.start()
     for to in around:
         pl.semaphore_signal(barrier, inc=1, device_id=to, device_id_type=MESH)
+    for copy in fetch[0:4]:
+        copy.wait()
 
     def first(i, _):
         for half in range(2):
@@ -295,20 +311,36 @@
     for copy in copies:
         copy.start()
 
+    for copy in fetch[4:]:
+        copy.wait()
     pair_coef[0:33, :] = jnp.dot(
         collision[...], selector[...], preferred_element_type=F32
     ).astype(BF)
     pair_coef[33:48, :] = jnp.zeros((15, PAIRS), BF)
-    across = jnp.broadcast_to(counts[...], (COLS, COLS)).astype(F32)
     i0 = lax.broadcasted_iota(jnp.int32, (COLS, COLS), 0)
     i1 = lax.broadcasted_iota(jnp.int32, (COLS, COLS), 1)
+    wide = jnp.concatenate([growth[...], jnp.zeros((1, COLS - BINS), F32)], axis=1)
+    growth_col[...] = jnp.broadcast_to(
+        jnp.sum(
+            jnp.where((i0 == i1)[0:ROWS], jnp.broadcast_to(wide, (ROWS, COLS)), 0.0), axis=1, keepdims=True
+        ),
+        (ROWS, COLS),
+    )
+    across = jnp.broadcast_to(counts[...], (COLS, COLS)).astype(F32)
     along = jnp.sum(jnp.where(i0 == i1, across, 0.0), axis=1, keepdims=True)
     before = (across > along) | ((across == along) & (i1 < i0))
-    place = jnp.sum(jnp.where(before, 1.0, 0.0), axis=1, keepdims=True)
-    place = jnp.broadcast_to(place, (COLS, COLS)).astype(jnp.int32)
-    rank[...] = place
-    listed = jnp.sum(jnp.where(place == i1, i0.astype(F32), 0.0), axis=0, keepdims=True)
-    order[...] = listed.astype(jnp.int32)
+    place = jnp.sum(jnp.where(before, 1.0, 0.0), axis=1, keepdims=True).astype(jnp.int32)
+    after = (along > across) | ((along == across) & (i0 < i1))
+    place_row = jnp.sum(jnp.where(after, 1.0, 0.0), axis=0, keepdims=True).astype(jnp.int32)
+    counts_out[...] = jnp.sum(jnp.where(place == i1, along, 0.0), axis=0, keepdims=True).astype(jnp.int32)
+    unsort[...] = jnp.where(place == i1, 1.0, 0.0).astype(BF)
+    sort = jnp.where(place_row == i0, 1.0, 0.0).astype(BF)
+    for b in range(BINS):
+        sorted_bin = jnp.dot(sort, drops[b], preferred_element_type=F32)
+        for half in range(2):
+            start[pl.ds(half * COLS * ROWS + b, COLS, stride=ROWS), :] = sorted_bin[
+                :, half * 128 : (half + 1) * 128
+            ]
 
     for copy in copies:
         copy.wait()
@@ -342,31 +374,43 @@
         for half in range(2)
     ]
     by_row = jnp.concatenate(parts, axis=1)
-    for e in range(2):
-        forcing = lax.dot_general(
+    forcing = [
+        lax.dot_general(
             col_map[...], by_row[16 * e : 16 * (e + 1)], (((1,), (1,)), ((), ())),
             precision=HIGH, preferred_element_type=F32,
         ).astype(BF)
-        cell_forcing[64 * e : 64 * (e + 1), :] = DT_CRM * jnp.dot(
-            forcing, cells[...], preferred_element_type=F32
-        )
-
-
-def dynamics(tracer, wind_x, wind_y, counts_row, collision):
+        for e in range(2)
+    ]
+    by_cell = jnp.dot(
+        jnp.concatenate(forcing, axis=0), cells[...], preferred_element_type=F32
+    ).astype(BF)
+    cell_forcing[...] = DT_CRM * jnp.dot(sort, by_cell, preferred_element_type=F32)
+
+
+def dynamics(tracer, wind_x, wind_y, drops, counts_row, growth_row, collision):
     row_map, col_map = forcing_tables()
     shape = tracer.shape
+    operands = (
+        tracer, wind_x, wind_y, drops, counts_row, growth_row, collision,
+        jnp.asarray(stencil_table()), jnp.asarray(pair_selector()),
+        jnp.asarray(row_map), jnp.asarray(col_map), jnp.asarray(spread_cells()),
+    )
     return pl.pallas_call(
         dynamics_kernel,
         out_shape=(
             jax.ShapeDtypeStruct(shape, F32),
             jax.ShapeDtypeStruct((COLS, 256), F32),
             jax.ShapeDtypeStruct((48, PAIRS), BF),
+            jax.ShapeDtypeStruct((ROWS, 128), F32),
+            jax.ShapeDtypeStruct((2 * COLS * ROWS, 128), F32),
             jax.ShapeDtypeStruct((1, COLS), jnp.int32),
-            jax.ShapeDtypeStruct((COLS, COLS), jnp.int32),
+            jax.ShapeDtypeStruct((COLS, COLS), BF),
         ),
-        in_specs=[VMEM] * 10,
-        out_specs=(VMEM,) * 5,
-        scratch_shapes=[
+        in_specs=[HBM] * 12,
+        out_specs=(VMEM,) * 7,
+        scratch_shapes=[pltpu.VMEM(x.shape, x.dtype) for x in operands]
+        + [
+            pltpu.SemaphoreType.DMA((12,)),
             pltpu.VMEM((2 * PTS, 128), F32),
             pltpu.VMEM((2 * PTS, 128), F32),
             pltpu.VMEM((2, 2, 8, 128), F32),
@@ -380,27 +424,26 @@
             collective_id=0, has_side_effects=True, vmem_limit_bytes=40 << 20
         ),
         name="dynamics",
-    )(
-        tracer, wind_x, wind_y, counts_row, collision,
-        jnp.asarray(stencil_table()), jnp.asarray(pair_selector()),
-        jnp.asarray(row_map), jnp.asarray(col_map), jnp.asarray(spread_cells()),
-    )
+    )(*operands)
 
 
 def micro_kernel(
-    order, counts, drops, cell_forcing, pair_coef, growth, group, rank,
+    counts, start, cell_forcing, pair_coef, growth, group, unsort,
     drops_next, heat_out, echo_out,
     cloud, doubled, grow, heat_rows, echo_rows,
 ):
-    mass = (lax.broadcasted_iota(jnp.int32, (40, 128), 0).astype(F32) + 1.0) / BINS
+    mass = (lax.broadcasted_iota(jnp.int32, (ROWS, 128), 0).astype(F32) + 1.0) / BINS
     srow = lax.broadcasted_iota(jnp.int32, (8, 128), 0)
+
+    def place(p, b, half):
+        return pl.ds(pl.multiple_of((half * COLS + p * BATCH + b) * ROWS, 8), ROWS)
 
     def substep(s, p):
         for b in range(BATCH):
-            active = s < counts[order[0, p * BATCH + b]]
+            active = s < counts[0, p * BATCH + b]
             blocks, grown, olds = [], [], []
             for half in range(2):
-                old = cloud[b, half]
+                old = cloud[place(p, b, half), :]
                 now = old + grow[b, half]
                 doubled[b, half, 0:32, :] = now[0:32]
                 doubled[b, half, 32:48, :] = now[0:16]
@@ -422,49 +465,40 @@
                 pair_coef[...], jnp.concatenate(blocks, axis=1), preferred_element_type=F32
             )
             for half in range(2):
-                moved = grown[half] + DT_CRM * change[0:40, half * 128 : (half + 1) * 128]
-                cloud[b, half] = jnp.where(active, moved, olds[half])
+                moved = grown[half] + DT_CRM * change[0:ROWS, half * 128 : (half + 1) * 128]
+                cloud[place(p, b, half), :] = jnp.where(active, moved, olds[half])
         return p
 
     def batch(p, _):
         for b in range(BATCH):
-            col = order[0, p * BATCH + b]
-            forced = cell_forcing[pl.ds(col, 1), :]
+            forced = cell_forcing[pl.ds(p * BATCH + b, 1), :]
             for half in range(2):
-                at = slice(half * 128, (half + 1) * 128)
-                cloud[b, half, 0:32, :] = drops[col, 0:32, at].astype(F32)
-                cloud[b, half, 32:40, :] = jnp.broadcast_to(drops[col, 32:33, at].astype(F32), (8, 128))
-                grow[b, half] = forced[:, at] * growth[...]
-        lax.fori_loop(0, counts[order[0, p * BATCH]], substep, p)
-        heats = [jnp.zeros((8, 128), F32)] * 2
-        echos = [jnp.zeros((8, 128), F32)] * 2
-        for b in range(BATCH):
-            col = order[0, p * BATCH + b]
-            for half in range(2):
-                at = slice(half * 128, (half + 1) * 128)
-                final = cloud[b, half]
-                drops_next[col, 0:32, at] = final[0:32].astype(BF)
-                drops_next[col, 32:33, at] = final[32:33].astype(BF)
-                gain = (final[0:32] - drops[col, 0:32, at].astype(F32)) * mass[0:32]
-                gain_last = (final[32:33] - drops[col, 32:33, at].astype(F32)) * mass[32:33]
-                weighed = final * mass
-                square = weighed * weighed
-                heats[half] = jnp.where(
-                    srow == b, jnp.sum(gain, axis=0, keepdims=True) + gain_last, heats[half]
-                )
-                echos[half] = jnp.where(
-                    srow == b, jnp.sum(square[0:32], axis=0, keepdims=True) + square[32:33], echos[half]
-                )
+                cloud[place(p, b, half), :] = start[place(p, b, half), :]
+                grow[b, half] = forced[:, half * 128 : (half + 1) * 128] * growth[...]
+        lax.fori_loop(0, counts[0, p * BATCH], substep, p)
         for half in range(2):
             at = slice(half * 128, (half + 1) * 128)
-            heat_rows[p, :, at] = heats[half]
-            echo_rows[p, :, at] = echos[half]
+            for eight in range(BATCH // 8):
+                heats = jnp.zeros((8, 128), F32)
+                echos = jnp.zeros((8, 128), F32)
+                for b in range(8):
+                    where = place(p, eight * 8 + b, half)
+                    final = cloud[where, :]
+                    gain = (final - start[where, :]) * mass
+                    weighed = final * mass
+                    square = weighed * weighed
+                    heats = jnp.where(
+                        srow == b, jnp.sum(gain[0:32], axis=0, keepdims=True) + gain[32:33], heats
+                    )
+                    echos = jnp.where(
+                        srow == b, jnp.sum(square[0:32], axis=0, keepdims=True) + square[32:33], echos
+                    )
+                rows = pl.ds(pl.multiple_of(p * BATCH + eight * 8, 8), 8)
+                heat_rows[rows, at] = heats
+                echo_rows[rows, at] = echos
         return 0
 
     lax.fori_loop(0, COLS // BATCH, batch, 0)
-    total = COLS // BATCH * 8
-    q = lax.broadcasted_iota(jnp.int32, (COLS, total), 1)
-    pick = ((q // 8 * BATCH + q % 8 == rank[:, 0:1]) & (q % 8 < BATCH)).astype(F32).astype(BF)
 
     def group_mean(x):
         acc = None
@@ -473,31 +507,37 @@
             acc = y if acc is None else acc + y
         return acc
 
-    heat = group_mean(heat_rows[...].reshape(total, 256)).astype(BF)
-    heat_out[...] = jnp.dot(pick, heat, preferred_element_type=F32).astype(BF)
-    echo_out[...] = jnp.log(1.0 + dot_exact(pick, group_mean(echo_rows[...].reshape(total, 256))))
-
-
-def microphysics(order, counts, drops, cell_forcing, pair_coef, growth, rank):
+    back = unsort[...]
+    heat = group_mean(heat_rows[...]).astype(BF)
+    heat_out[...] = jnp.dot(back, heat, preferred_element_type=F32).astype(BF)
+    echo_out[...] = jnp.log(1.0 + dot_exact(back, group_mean(echo_rows[...])))
+    for b in range(BINS):
+        halves = [cloud[pl.ds(half * COLS * ROWS + b, COLS, stride=ROWS), :] for half in range(2)]
+        drops_next[b] = jnp.dot(
+            back, jnp.concatenate(halves, axis=1).astype(BF), preferred_element_type=F32
+        ).astype(BF)
+
+
+def microphysics(counts, start, cell_forcing, pair_coef, growth, unsort):
     return pl.pallas_call(
         micro_kernel,
         out_shape=(
-            jax.ShapeDtypeStruct(drops.shape, BF),
+            jax.ShapeDtypeStruct((BINS, COLS, 256), BF),
             jax.ShapeDtypeStruct((COLS, 128), BF),
             jax.ShapeDtypeStruct((COLS, 128), F32),
         ),
-        in_specs=[SMEM, SMEM] + [VMEM] * 6,
+        in_specs=[SMEM] + [VMEM] * 6,
         out_specs=(VMEM,) * 3,
         scratch_shapes=[
-            pltpu.VMEM((BATCH, 2, 40, 128), F32),
+            pltpu.VMEM((2 * COLS * ROWS, 128), F32),
             pltpu.VMEM((BATCH, 2, 48, 128), F32),
-            pltpu.VMEM((BATCH, 2, 40, 128), F32),
-            pltpu.VMEM((COLS // BATCH, 8, 256), F32),
-            pltpu.VMEM((COLS // BATCH, 8, 256), F32),
+            pltpu.VMEM((BATCH, 2, ROWS, 128), F32),
+            pltpu.VMEM((COLS, 256), F32),
+            pltpu.VMEM((COLS, 256), F32),
         ],
         compiler_params=pltpu.CompilerParams(vmem_limit_bytes=40 << 20),
         name="microphysics",
-    )(order, counts, drops, cell_forcing, pair_coef, growth, jnp.asarray(group_matrix()), rank)
+    )(counts, start, cell_forcing, pair_coef, growth, jnp.asarray(group_matrix()), unsort)
 
 
 def coupling_kernel(
@@ -650,15 +690,15 @@
 
 
 def shards(tracer, wind_x, wind_y, drops, owner, counts, collision, growth):
-    state, cell_forcing, pair_coef, order, rank = dynamics(
-        tracer, wind_x, wind_y, counts.reshape(1, COLS), collision
+    state, cell_forcing, pair_coef, growth_col, start, sorted_counts, unsort = dynamics(
+        tracer, wind_x, wind_y, drops.transpose(1, 0, 2),
+        counts.reshape(1, COLS), growth.reshape(1, BINS), collision,
     )
-    column = jnp.broadcast_to(jnp.pad(growth, (0, 7))[:, None], (40, 128))
     drops_next, heat, echo = microphysics(
-        order, counts, drops, cell_forcing, pair_coef, column, rank
+        sorted_counts, start, cell_forcing, pair_coef, growth_col, unsort
     )
     tracer_next, power = coupling(state, heat, echo, owner.reshape(1, COLS))
-    return (tracer_next, drops_next, power)
+    return (tracer_next, drops_next.transpose(1, 0, 2), power)
 
 
 def solution(mesh):

time: 99.7 us -> 91.1 us (0.914)
  Pallas kernels: 82.7 us -> 75.7 us
  local copies, waits for them, and re-layouts: 14.6 us -> 13 us
    pallas_call x1, Pallas kernels: 48.4 us -> 39.4 us  [coupling(): pl.pallas_call(coupling_kernel, out_shape=(jax.ShapeDtypeStruct(state.sha...]
    pallas_call x1, Pallas kernels: 24.1 us -> 25.5 us  [dynamics(): pl.pallas_call(dynamics_kernel, out_shape=(jax.ShapeDtypeStruct(shape, F3...]
    unnamed x38 -> x36, local copies, waits for them, and re-layouts: 13.9 us -> 13 us
where the time goes in v2:
time: 91.1 us; the launch traced here: 89.5 us
  Pallas kernels  75.7 us (83%)
  local copies, waits for them, and re-layouts  13 us (14%)
    pallas_call x1, Pallas kernels, coupling(): pl.pallas_call(coupling_kernel, out_shape=(jax.ShapeDtypeStruct(state.sha...  39.4 us
    pallas_call x1, Pallas kernels, dynamics(): pl.pallas_call(dynamics_kernel, out_shape=(jax.ShapeDtypeStruct(shape, F3...  25.5 us
    unnamed x36, local copies, waits for them, and re-layouts  13 us
    pallas_call x1, Pallas kernels, microphysics(): pl.pallas_call(micro_kernel, out_shape=(jax.ShapeDtypeStruct((BINS, COLS,...  10.9 us

profile of v2, /device:TPU:0, one launch (start us, length us, event | category | flops | bytes accessed | tf_op | source)
XLA Modules:
  0.0 89.5 jit_solution(6731759733523696964)
XLA Ops:
  0.6 0.0 copy-start
  0.6 1.6 %copy-done = bf16[128,33,256]{2,0,1:T(8,128)(2,1)S(1)} copy-done((bf16[128,33,256]{2,0,1:T(8,128)(2,1)S(1)}, bf16[128,33,256]{2,0,1:T(8,128)(2,1)}, u32[]{:S(2)}) %copy-start) | copy-done | bytes 2162712
  2.2 1.3 %copy-done.1 = bf16[1089,576]{1,0:T(8,128)(2,1)S(1)} copy-done((bf16[1089,576]{1,0:T(8,128)(2,1)S(1)}, bf16[1089,576]{1,0:T(8,128)(2,1)}, u32[]{:S(2)}) %copy-start.1) | copy-done | bytes 1254552
  3.6 1.1 %copy-done.2 = f32[72,8,256]{2,1,0:T(8,128)S(1)} copy-done((f32[72,8,256]{2,1,0:T(8,128)S(1)}, f32[72,8,256]{2,1,0:T(8,128)}, u32[]{:S(2)}) %copy-start.2) | copy-done | bytes 589848
  4.7 1.1 %copy-done.3 = f32[72,8,256]{2,1,0:T(8,128)S(1)} copy-done((f32[72,8,256]{2,1,0:T(8,128)S(1)}, f32[72,8,256]{2,1,0:T(8,128)}, u32[]{:S(2)}) %copy-start.3) | copy-done | bytes 589848
  5.7 1.1 %copy-done.4 = f32[72,8,256]{2,1,0:T(8,128)S(1)} copy-done((f32[72,8,256]{2,1,0:T(8,128)S(1)}, f32[72,8,256]{2,1,0:T(8,128)}, u32[]{:S(2)}) %copy-start.4) | copy-done | bytes 589848
  6.8 0.9 copy-done.7
  7.7 0.9 copy-done.8
  8.6 0.8 copy-done.10
  9.4 0.8 copy-done.11
  10.2 0.7 copy-done.13
  10.9 0.7 copy-done.15
  11.6 0.7 copy-done.16
  12.2 25.5 %dynamics.1 = (f32[72,8,256]{2,1,0:T(8,128)S(1)}, f32[128,256]{1,0:T(8,128)S(1)}, bf16[48,576]{1,0:T(8,128)(2,1)S(1)}, f32[40,128]{1,0:T(8,128)S(1)}, f32[10240,...) custom-call(f32[72,8,256]{2,1,0:T(8,128)S(1)} %copy-done.2, f32[72,8,256]{2,1,0:T(8,128)S(1)} %copy-done.3, ...), custom_call_target="tpu_custom_call" | custom-call | tf_op jit(solution)/shard_map/dynamics/pallas_call | solution.py:398
  37.7 0.0 copy-done.9
  37.7 0.0 copy-start.5
  37.7 0.0 copy-start.6
  37.8 0.0 copy-start.12
  37.8 0.0 copy-start.14
  37.8 10.9 %microphysics.1 = (bf16[33,128,256]{2,1,0:T(8,128)(2,1)}, bf16[128,128]{1,0:T(8,128)(2,1)S(1)}, f32[128,128]{1,0:T(8,128)S(1)}) custom-call(s32[1,128]{1,0:T(1,128)S(1)} %get-tuple-element.16.counts, f32[10240,128]{1,0:T(8,128)S(1)} %get-tuple-element.17.start, f32[128,256]{1,0:T(8,128)S(1)} %get-tuple-element.18.cell_forcing, ...), custom_call_target="tpu_custom_call" | custom-call | tf_op jit(solution)/shard_map/microphysics/pallas_call | solution.py:522
  48.7 0.0 copy-done.6
  48.7 39.4 %coupling.1 = (f32[72,8,256]{2,1,0:T(8,128)S(1)}, f32[16,256]{1,0:T(8,128)S(1)}) custom-call(f32[72,8,256]{2,1,0:T(8,128)S(1)} %get-tuple-element.15.state, bf16[128,128]{1,0:T(8,128)(2,1)S(1)} %get-tuple-element.22.heat, f32[128,128]{1,0:T(8,128)S(1)} %get-tuple-element.23.echo, s32[1,128]{1,0:T(1,128)S(1)} %bitcast.6, bf16[576,64]{1,0:T(8,128)(2,1)S(1)} %copy-done.5, ...), custom_call_target="tpu_custom_call" | custom-call | tf_op jit(solution)/shard_map/coupling/pallas_call | solution.py:657
  88.1 0.8 copy.22
  88.9 0.6 copy.23
  (15 shorter events, 0.0 us)
Async XLA Ops:
  0.6 1.6 %copy-start = (bf16[128,33,256]{2,0,1:T(8,128)(2,1)S(1)}, bf16[128,33,256]{2,0,1:T(8,128)(2,1)}, u32[]{:S(2)}) copy-start(bf16[128,33,256]{2,0,1:T(8,128)(2,1)} %param.20) | copy-start | bytes 6488068
  2.2 1.3 %copy-start.1 = (bf16[1089,576]{1,0:T(8,128)(2,1)S(1)}, bf16[1089,576]{1,0:T(8,128)(2,1)}, u32[]{:S(2)}) copy-start(bf16[1089,576]{1,0:T(8,128)(2,1)} %constant.19.clone.selector_h) | copy-start | bytes 3763588
  3.6 1.1 %copy-start.2 = (f32[72,8,256]{2,1,0:T(8,128)S(1)}, f32[72,8,256]{2,1,0:T(8,128)}, u32[]{:S(2)}) copy-start(f32[72,8,256]{2,1,0:T(8,128)} %tracer_h.1) | copy-start | bytes 1769476
  4.7 1.1 %copy-start.3 = (f32[72,8,256]{2,1,0:T(8,128)S(1)}, f32[72,8,256]{2,1,0:T(8,128)}, u32[]{:S(2)}) copy-start(f32[72,8,256]{2,1,0:T(8,128)} %wind_x_h.1) | copy-start | bytes 1769476
  5.7 1.1 %copy-start.4 = (f32[72,8,256]{2,1,0:T(8,128)S(1)}, f32[72,8,256]{2,1,0:T(8,128)}, u32[]{:S(2)}) copy-start(f32[72,8,256]{2,1,0:T(8,128)} %wind_y_h.1) | copy-start | bytes 1769476
  6.8 0.9 copy-start.7
  7.7 0.9 copy-start.8
  8.6 0.8 copy-start.10
  9.4 0.8 copy-start.11
  10.2 0.7 copy-start.13
  10.9 0.7 copy-start.15
  11.6 0.7 copy-start.16
  12.2 25.5 %copy-start.9 = (bf16[256,128]{1,0:T(8,128)(2,1)S(1)}, bf16[256,128]{1,0:T(8,128)(2,1)}, u32[]{:S(2)}) copy-start(bf16[256,128]{1,0:T(8,128)(2,1)} %constant.23.clone.group) | copy-start | bytes 196612
  37.7 10.9 %copy-start.5 = (bf16[576,64]{1,0:T(8,128)(2,1)S(1)}, bf16[576,64]{1,0:T(8,128)(2,1)}, u32[]{:S(2)}) copy-start(bf16[576,64]{1,0:T(8,128)(2,1)} %constant.24.clone.heating) | copy-start | bytes 221188
  37.7 10.9 %copy-start.6 = (bf16[256,256]{1,0:T(8,128)(2,1)S(1)}, bf16[256,256]{1,0:T(8,128)(2,1)}, u32[]{:S(2)}) copy-start(bf16[256,256]{1,0:T(8,128)(2,1)} %constant.26.clone.slots) | copy-start | bytes 393220
  37.8 10.9 %copy-start.12 = (bf16[64,256]{1,0:T(8,128)(2,1)S(1)}, bf16[64,256]{1,0:T(8,128)(2,1)}, u32[]{:S(2)}) copy-start(bf16[64,256]{1,0:T(8,128)(2,1)} %constant.25.clone.spread) | copy-start | bytes 98308
  37.8 10.9 %copy-start.14 = (s32[128,1]{0,1:T(1,128)S(1)}, s32[128,1]{0,1:T(1,128)}, u32[]{:S(2)}) copy-start(s32[128,1]{0,1:T(1,128)} %param.21) | copy-start | bytes 1540

commit v3 on v2

--- a/solution.py
+++ b/solution.py
@@ -424,7 +424,7 @@
             collective_id=0, has_side_effects=True, vmem_limit_bytes=40 << 20
         ),
         name="dynamics",
-    )(*operands)
+    )(*[pltpu.with_memory_space_constraint(x, pltpu.HBM) for x in operands])
 
 
 def micro_kernel(

time: 91.1 us -> 77.8 us (0.85)
  local copies, waits for them, and re-layouts: 13 us -> 1.46 us
  Pallas kernels: 75.7 us -> 74.5 us
    unnamed x36 -> x12, local copies, waits for them, and re-layouts: 13 us -> 1.46 us
    pallas_call x1, Pallas kernels: 25.5 us -> 24.4 us  [dynamics(): pl.pallas_call(dynamics_kernel, out_shape=(jax.ShapeDtypeStruct(shape, F3...]
    pallas_call x1, Pallas kernels: 10.9 us -> 9.89 us  [microphysics(): pl.pallas_call(micro_kernel, out_shape=(jax.ShapeDtypeStruct((BINS, COLS,...]
where the time goes in v3:
time: 77.8 us; the launch traced here: 76.6 us
  Pallas kernels  74.5 us (96%)
  local copies, waits for them, and re-layouts  1.46 us (2%)
    pallas_call x1, Pallas kernels, coupling(): pl.pallas_call(coupling_kernel, out_shape=(jax.ShapeDtypeStruct(state.sha...  40.2 us
    pallas_call x1, Pallas kernels, dynamics(): pl.pallas_call(dynamics_kernel, out_shape=(jax.ShapeDtypeStruct(shape, F3...  24.4 us
    pallas_call x1, Pallas kernels, microphysics(): pl.pallas_call(micro_kernel, out_shape=(jax.ShapeDtypeStruct((BINS, COLS,...  9.89 us

profile of v3, /device:TPU:0, one launch (start us, length us, event | category | flops | bytes accessed | tf_op | source)
XLA Modules:
  0.0 76.6 jit_solution(4349445738249395556)
XLA Ops:
  0.6 0.0 copy-start.2
  0.6 24.4 %dynamics.1 = (f32[72,8,256]{2,1,0:T(8,128)S(1)}, f32[128,256]{1,0:T(8,128)S(1)}, bf16[48,576]{1,0:T(8,128)(2,1)S(1)}, f32[40,128]{1,0:T(8,128)S(1)}, f32[10240,...) custom-call(f32[72,8,256]{2,1,0:T(8,128)} %tracer_h.1, f32[72,8,256]{2,1,0:T(8,128)} %wind_x_h.1, ...), custom_call_target="tpu_custom_call" | custom-call | tf_op jit(solution)/shard_map/dynamics/pallas_call | solution.py:398
  25.0 0.0 copy-done.2
  25.0 0.0 copy-start
  25.1 0.0 copy-start.1
  25.1 0.0 copy-start.3
  25.1 0.0 copy-start.4
  25.1 9.9 %microphysics.1 = (bf16[33,128,256]{2,1,0:T(8,128)(2,1)}, bf16[128,128]{1,0:T(8,128)(2,1)S(1)}, f32[128,128]{1,0:T(8,128)S(1)}) custom-call(s32[1,128]{1,0:T(1,128)S(1)} %get-tuple-element.16.counts, f32[10240,128]{1,0:T(8,128)S(1)} %get-tuple-element.17.start, f32[128,256]{1,0:T(8,128)S(1)} %get-tuple-element.18.cell_forcing, ...), custom_call_target="tpu_custom_call" | custom-call | tf_op jit(solution)/shard_map/microphysics/pallas_call | solution.py:522
  35.0 0.0 copy-done
  35.0 0.0 copy-done.1
  35.0 0.0 copy-done.3
  35.0 0.0 copy-done.4
  35.0 40.2 %coupling.1 = (f32[72,8,256]{2,1,0:T(8,128)S(1)}, f32[16,256]{1,0:T(8,128)S(1)}) custom-call(f32[72,8,256]{2,1,0:T(8,128)S(1)} %get-tuple-element.15.state, bf16[128,128]{1,0:T(8,128)(2,1)S(1)} %get-tuple-element.22.heat, f32[128,128]{1,0:T(8,128)S(1)} %get-tuple-element.23.echo, s32[1,128]{1,0:T(1,128)S(1)} %bitcast.5, bf16[576,64]{1,0:T(8,128)(2,1)S(1)} %copy-done, ...), custom_call_target="tpu_custom_call" | custom-call | tf_op jit(solution)/shard_map/coupling/pallas_call | solution.py:657
  75.2 0.8 %copy.22 = f32[72,8,256]{2,1,0:T(8,128)} copy(f32[72,8,256]{2,1,0:T(8,128)S(1)} %get-tuple-element.30) | data formatting | bytes 1179648
  76.0 0.6 copy.23
Async XLA Ops:
  0.6 24.4 %copy-start.2 = (bf16[256,128]{1,0:T(8,128)(2,1)S(1)}, bf16[256,128]{1,0:T(8,128)(2,1)}, u32[]{:S(2)}) copy-start(bf16[256,128]{1,0:T(8,128)(2,1)} %constant.23.clone.group) | copy-start | bytes 196612
  25.0 9.9 %copy-start = (bf16[576,64]{1,0:T(8,128)(2,1)S(1)}, bf16[576,64]{1,0:T(8,128)(2,1)}, u32[]{:S(2)}) copy-start(bf16[576,64]{1,0:T(8,128)(2,1)} %constant.24.clone.heating) | copy-start | bytes 221188
  25.1 9.9 %copy-start.1 = (bf16[256,256]{1,0:T(8,128)(2,1)S(1)}, bf16[256,256]{1,0:T(8,128)(2,1)}, u32[]{:S(2)}) copy-start(bf16[256,256]{1,0:T(8,128)(2,1)} %constant.26.clone.slots) | copy-start | bytes 393220
  25.1 9.9 %copy-start.3 = (bf16[64,256]{1,0:T(8,128)(2,1)S(1)}, bf16[64,256]{1,0:T(8,128)(2,1)}, u32[]{:S(2)}) copy-start(bf16[64,256]{1,0:T(8,128)(2,1)} %constant.25.clone.spread) | copy-start | bytes 98308
  25.1 9.9 %copy-start.4 = (s32[128,1]{0,1:T(1,128)S(1)}, s32[128,1]{0,1:T(1,128)}, u32[]{:S(2)}) copy-start(s32[128,1]{0,1:T(1,128)} %param.21) | copy-start | bytes 1540

commit v4 on v3

--- a/solution.py
+++ b/solution.py
@@ -28,7 +28,7 @@
 DT_DYN = 0.04
 DT_CRM = 0.05
 DT_PHYS = 0.5
-BATCH = 16
+BATCH = 32
 ROWS = 40
 
 
@@ -56,15 +56,18 @@
     return (down_map, up_map)
 
 
-def stencil_table():
+def stencil_tables():
     derivative, _ = gll_tables()
-    out = np.zeros((14, 8, 128), np.float32)
-    for s in range(-3, 4):
-        for i in range(4):
-            if 0 <= i + s < 4:
-                out[s + 3, i::4, :] = -derivative[i, i + s]
-                out[s + 10, :, i::4] = -derivative[i, i + s]
-    return out
+    out = []
+    for size in (64, 128):
+        whole = np.kron(np.eye(size // 4), -derivative).astype(np.float32)
+        if size == 128:
+            whole = whole.T
+        near = whole.astype(ml_dtypes.bfloat16)
+        out += [near, (whole - near.astype(np.float32)).astype(ml_dtypes.bfloat16)]
+    by_rows = np.concatenate([out[0], out[0], out[1]], axis=1)
+    by_cols = np.block([[out[2], out[3]], [out[2], np.zeros_like(out[2])]])
+    return by_rows, by_cols
 
 
 def forcing_tables():
@@ -156,13 +159,16 @@
     return acc
 
 
-def tendency(q, wind_x, wind_y, table):
-    grad_x = table[3][None] * q
-    grad_y = table[10][None] * q
-    for s in (-3, -2, -1, 1, 2, 3):
-        grad_x = grad_x + table[s + 3][None] * pltpu.roll(q, (-s) % 8, 1)
-        grad_y = grad_y + table[s + 10][None] * pltpu.roll(q, (-s) % 128, 2)
-    return wind_x * grad_x + wind_y * grad_y
+def tendency(q, wind_x, wind_y, by_rows, by_cols):
+    near = q.astype(BF)
+    rest = (q - near.astype(F32)).astype(BF)
+    grad_x = jnp.dot(by_rows, jnp.concatenate([near, rest, near], axis=0), preferred_element_type=F32)
+    grad_y = []
+    for at in (slice(0, 128), slice(128, 256)):
+        both = jnp.concatenate([near[:, at], rest[:, at]], axis=1)
+        y = jnp.dot(both, by_cols, preferred_element_type=F32)
+        grad_y.append(y[:, 0:128] + y[:, 128:256])
+    return wind_x * grad_x + wind_y * jnp.concatenate(grad_y, axis=1)
 
 
 def neighbours():
@@ -212,13 +218,23 @@
         pltpu.make_async_remote_copy(
             src_ref=src,
             dst_ref=dst,
-            send_sem=send.at[n],
-            recv_sem=recv.at[n],
+            send_sem=send.at[0 if n < 2 else 1],
+            recv_sem=recv.at[0 if n < 2 else 1],
             device_id=to,
             device_id_type=MESH,
         )
         for n, (src, dst, to) in enumerate(plan)
     ]
+
+
+def wait_bytes(ref, sem):
+    pltpu.make_async_copy(ref, ref, sem).wait()
+
+
+def halo_wait(got_packs, got_rows, send, recv):
+    for sems in (recv, send):
+        wait_bytes(got_rows, sems.at[0])
+        wait_bytes(got_packs, sems.at[1])
 
 
 def assemble_loop(field, got_packs, got_rows, use):
@@ -257,34 +273,43 @@
         halo_r = jnp.stack([pltpu.roll(right_c, 127 - k, 1) for k in range(8)])
         near_l = [jnp.where(first, halo_l, lefts[0]), jnp.where(first, lefts[0], lefts[1])]
         near_r = [jnp.where(last, rights[1], rights[0]), jnp.where(last, halo_r, rights[1])]
+        done = []
         for half in range(2):
             m = means[half]
             other = jnp.where(lane3, near_r[half], jnp.where(lane0, near_l[half], m))
-            use(i, half, 0.5 * (m + other))
+            done.append((0.5 * (m + other)).reshape(64, 128))
+        use(i, done)
         return pltpu.roll(left_c, 120, 1), pltpu.roll(right_c, 120, 1)
 
     lax.fori_loop(0, 9, one, (left_halo, right_halo))
 
 
-def chunk_of(ref, i, half):
-    return ref[pl.ds(i * 8, 8), :, half * 128 : (half + 1) * 128]
+def chunk_of(ref, i):
+    return ref[pl.ds(i * 8, 8), :, :].reshape(64, 256)
+
+
+def put_halves(ref, i, x):
+    for half in range(2):
+        at = pl.multiple_of(half * PTS + i * 64, 64)
+        ref[pl.ds(at, 64), :] = x[:, half * 128 : (half + 1) * 128]
 
 
 def dynamics_kernel(
-    tracer_h, wind_x_h, wind_y_h, drops_h, counts_h, growth_h, collision_h, table_h, selector_h,
-    row_map_h, col_map_h, cells_h,
-    state, cell_forcing, pair_coef, growth_col, start, counts_out, unsort,
-    tracer, wind_x, wind_y, drops, counts, growth, collision, table, selector, row_map, col_map, cells,
+    tracer_h, wind_x_h, wind_y_h, drops_h, counts_h, growth_h, collision_h, by_rows_h, by_cols_h, selector_h,
+    row_map_h, col_map_h, cells_h, owner_h,
+    state, cell_forcing, pair_coef, growth_col, start, counts_out, unsort, sender,
+    tracer, wind_x, wind_y, drops, counts, growth, collision, by_rows, by_cols, selector,
+    row_map, col_map, cells, owner,
     loads, field, total, packs, rows, got_packs, got_rows, send, recv,
 ):
     g, c, up, down, left, right = neighbours()
     barrier = pltpu.get_barrier_semaphore()
     around = [(up, c), (down, c)]
     around += [(r, s) for s in (left, right) for r in (g, up, down)]
-    sources = [table_h, tracer_h, wind_x_h, wind_y_h, counts_h, growth_h, collision_h, selector_h, drops_h,
-               row_map_h, col_map_h, cells_h]
-    targets = [table, tracer, wind_x, wind_y, counts, growth, collision, selector, drops,
-               row_map, col_map, cells]
+    sources = [tracer_h, by_rows_h, by_cols_h, wind_x_h, wind_y_h, drops_h, counts_h, owner_h, collision_h,
+               selector_h, growth_h, row_map_h, col_map_h, cells_h]
+    targets = [tracer, by_rows, by_cols, wind_x, wind_y, drops, counts, owner, collision,
+               selector, growth, row_map, col_map, cells]
     fetch = [
         pltpu.make_async_copy(source, target, loads.at[n])
         for n, (source, target) in enumerate(zip(sources, targets))
@@ -293,25 +318,28 @@
         copy.start()
     for to in around:
         pl.semaphore_signal(barrier, inc=1, device_id=to, device_id_type=MESH)
-    for copy in fetch[0:4]:
+    for copy in fetch[0:5]:
         copy.wait()
 
-    def first(i, _):
-        for half in range(2):
-            t = tendency(
-                chunk_of(tracer, i, half), chunk_of(wind_x, i, half), chunk_of(wind_y, i, half), table
+    def first(n, _):
+        for k in range(3):
+            i = n * 3 + k
+            put_halves(
+                field, i,
+                tendency(
+                    chunk_of(tracer, i), chunk_of(wind_x, i), chunk_of(wind_y, i), by_rows[...], by_cols[...]
+                ),
             )
-            field[pl.ds(pl.multiple_of(half * PTS + i * 64, 64), 64), :] = t.reshape(64, 128)
         return 0
 
-    lax.fori_loop(0, 9, first, 0)
+    lax.fori_loop(0, 3, first, 0)
     pack_edges(field, packs.at[0], rows.at[0])
     pl.semaphore_wait(barrier, 8)
     copies = halo_copies(packs.at[0], rows.at[0], got_packs.at[0], got_rows.at[0], send.at[0], recv.at[0])
     for copy in copies:
         copy.start()
 
-    for copy in fetch[4:]:
+    for copy in fetch[5:]:
         copy.wait()
     pair_coef[0:33, :] = jnp.dot(
         collision[...], selector[...], preferred_element_type=F32
@@ -342,31 +370,43 @@
                 :, half * 128 : (half + 1) * 128
             ]
 
-    for copy in copies:
-        copy.wait()
-
-    def second(i, half, mean):
-        at = pl.multiple_of(half * PTS + i * 64, 64)
-        moved = chunk_of(tracer, i, half) + DT_DYN * mean
-        state[pl.ds(i * 8, 8), :, half * 128 : (half + 1) * 128] = moved
-        total[pl.ds(at, 64), :] = mean.reshape(64, 128)
-        t = tendency(moved, chunk_of(wind_x, i, half), chunk_of(wind_y, i, half), table)
-        field[pl.ds(at, 64), :] = t.reshape(64, 128)
+    for b in range(BINS, ROWS):
+        for half in range(2):
+            start[pl.ds(half * COLS * ROWS + b, COLS, stride=ROWS), :] = jnp.zeros((COLS, 128), F32)
+    owners = jnp.broadcast_to(owner[...], (COLS, COLS))
+    owned = jnp.sum(jnp.where(i0 == i1, owners.astype(F32), 0.0), axis=1, keepdims=True)
+    earlier = (owned == owners.astype(F32)) & (i0 < i1)
+    turn = jnp.sum(jnp.where(earlier, 1.0, 0.0), axis=0, keepdims=True)
+    key = owners % NC * NG + owners // NC
+    sender[...] = jnp.concatenate(
+        [jnp.where((key == i0) & (turn == float(r)), 1.0, 0.0) for r in range(2)], axis=1
+    ).astype(BF)
+
+    halo_wait(got_packs.at[0], got_rows.at[0], send.at[0], recv.at[0])
+
+    def second(i, means):
+        mean = jnp.concatenate(means, axis=1)
+        moved = chunk_of(tracer, i) + DT_DYN * mean
+        state[pl.ds(i * 8, 8), :, :] = moved.reshape(8, 8, 256)
+        put_halves(total, i, mean)
+        put_halves(
+            field, i,
+            tendency(moved, chunk_of(wind_x, i), chunk_of(wind_y, i), by_rows[...], by_cols[...]),
+        )
 
     assemble_loop(field, got_packs.at[0], got_rows.at[0], second)
     pack_edges(field, packs.at[1], rows.at[1])
     copies = halo_copies(packs.at[1], rows.at[1], got_packs.at[1], got_rows.at[1], send.at[1], recv.at[1])
     for copy in copies:
         copy.start()
-    for copy in copies:
-        copy.wait()
-
-    def third(i, half, mean):
-        at = pl.multiple_of(half * PTS + i * 64, 64)
-        state[pl.ds(i * 8, 8), :, half * 128 : (half + 1) * 128] = (
-            chunk_of(state, i, half) + DT_DYN * mean
-        )
-        total[pl.ds(at, 64), :] = total[pl.ds(at, 64), :] + mean.reshape(64, 128)
+    halo_wait(got_packs.at[1], got_rows.at[1], send.at[1], recv.at[1])
+
+    def third(i, means):
+        mean = jnp.concatenate(means, axis=1)
+        state[pl.ds(i * 8, 8), :, :] = (chunk_of(state, i) + DT_DYN * mean).reshape(8, 8, 256)
+        for half in range(2):
+            at = pl.multiple_of(half * PTS + i * 64, 64)
+            total[pl.ds(at, 64), :] = total[pl.ds(at, 64), :] + means[half]
 
     assemble_loop(field, got_packs.at[1], got_rows.at[1], third)
     parts = [
@@ -387,13 +427,14 @@
     cell_forcing[...] = DT_CRM * jnp.dot(sort, by_cell, preferred_element_type=F32)
 
 
-def dynamics(tracer, wind_x, wind_y, drops, counts_row, growth_row, collision):
+def dynamics(tracer, wind_x, wind_y, drops, counts_row, growth_row, collision, owner_row):
     row_map, col_map = forcing_tables()
+    by_rows, by_cols = stencil_tables()
     shape = tracer.shape
     operands = (
         tracer, wind_x, wind_y, drops, counts_row, growth_row, collision,
-        jnp.asarray(stencil_table()), jnp.asarray(pair_selector()),
-        jnp.asarray(row_map), jnp.asarray(col_map), jnp.asarray(spread_cells()),
+        jnp.asarray(by_rows), jnp.asarray(by_cols), jnp.asarray(pair_selector()),
+        jnp.asarray(row_map), jnp.asarray(col_map), jnp.asarray(spread_cells()), owner_row,
     )
     return pl.pallas_call(
         dynamics_kernel,
@@ -405,20 +446,21 @@
             jax.ShapeDtypeStruct((2 * COLS * ROWS, 128), F32),
             jax.ShapeDtypeStruct((1, COLS), jnp.int32),
             jax.ShapeDtypeStruct((COLS, COLS), BF),
+            jax.ShapeDtypeStruct((COLS, 2 * COLS), BF),
         ),
-        in_specs=[HBM] * 12,
-        out_specs=(VMEM,) * 7,
+        in_specs=[HBM] * 14,
+        out_specs=(VMEM,) * 8,
         scratch_shapes=[pltpu.VMEM(x.shape, x.dtype) for x in operands]
         + [
-            pltpu.SemaphoreType.DMA((12,)),
+            pltpu.SemaphoreType.DMA((14,)),
             pltpu.VMEM((2 * PTS, 128), F32),
             pltpu.VMEM((2 * PTS, 128), F32),
             pltpu.VMEM((2, 2, 8, 128), F32),
             pltpu.VMEM((2, 2, 2 * LEV, 128), F32),
             pltpu.VMEM((2, 6, 8, 128), F32),
             pltpu.VMEM((2, 2, 2 * LEV, 128), F32),
-            pltpu.SemaphoreType.DMA((2, 8)),
-            pltpu.SemaphoreType.DMA((2, 8)),
+            pltpu.SemaphoreType.DMA((2, 2)),
+            pltpu.SemaphoreType.DMA((2, 2)),
         ],
         compiler_params=pltpu.CompilerParams(
             collective_id=0, has_side_effects=True, vmem_limit_bytes=40 << 20
@@ -430,9 +472,10 @@
 def micro_kernel(
     counts, start, cell_forcing, pair_coef, growth, group, unsort,
     drops_next, heat_out, echo_out,
-    cloud, doubled, grow, heat_rows, echo_rows,
+    cloud, doubled, grow, heat_rows, echo_rows, drops_out, stores,
 ):
-    mass = (lax.broadcasted_iota(jnp.int32, (ROWS, 128), 0).astype(F32) + 1.0) / BINS
+    bins = lax.broadcasted_iota(jnp.int32, (ROWS, 128), 0)
+    mass = jnp.where(bins < BINS, (bins.astype(F32) + 1.0) / BINS, 0.0)
     srow = lax.broadcasted_iota(jnp.int32, (8, 128), 0)
 
     def place(p, b, half):
@@ -487,12 +530,8 @@
                     gain = (final - start[where, :]) * mass
                     weighed = final * mass
                     square = weighed * weighed
-                    heats = jnp.where(
-                        srow == b, jnp.sum(gain[0:32], axis=0, keepdims=True) + gain[32:33], heats
-                    )
-                    echos = jnp.where(
-                        srow == b, jnp.sum(square[0:32], axis=0, keepdims=True) + square[32:33], echos
-                    )
+                    heats = jnp.where(srow == b, jnp.sum(gain, axis=0, keepdims=True), heats)
+                    echos = jnp.where(srow == b, jnp.sum(square, axis=0, keepdims=True), echos)
                 rows = pl.ds(pl.multiple_of(p * BATCH + eight * 8, 8), 8)
                 heat_rows[rows, at] = heats
                 echo_rows[rows, at] = echos
@@ -508,14 +547,22 @@
         return acc
 
     back = unsort[...]
+    pieces = []
+    for n in range(3):
+        for b in range(11 * n, 11 * n + 11):
+            halves = [cloud[pl.ds(half * COLS * ROWS + b, COLS, stride=ROWS), :] for half in range(2)]
+            drops_out[b] = jnp.dot(
+                back, jnp.concatenate(halves, axis=1).astype(BF), preferred_element_type=F32
+            ).astype(BF)
+        part = pl.ds(11 * n, 11)
+        piece = pltpu.make_async_copy(drops_out.at[part], drops_next.at[part], stores.at[n])
+        piece.start()
+        pieces.append(piece)
     heat = group_mean(heat_rows[...]).astype(BF)
     heat_out[...] = jnp.dot(back, heat, preferred_element_type=F32).astype(BF)
     echo_out[...] = jnp.log(1.0 + dot_exact(back, group_mean(echo_rows[...])))
-    for b in range(BINS):
-        halves = [cloud[pl.ds(half * COLS * ROWS + b, COLS, stride=ROWS), :] for half in range(2)]
-        drops_next[b] = jnp.dot(
-            back, jnp.concatenate(halves, axis=1).astype(BF), preferred_element_type=F32
-        ).astype(BF)
+    for piece in pieces:
+        piece.wait()
 
 
 def microphysics(counts, start, cell_forcing, pair_coef, growth, unsort):
@@ -527,13 +574,15 @@
             jax.ShapeDtypeStruct((COLS, 128), F32),
         ),
         in_specs=[SMEM] + [VMEM] * 6,
-        out_specs=(VMEM,) * 3,
+        out_specs=(HBM, VMEM, VMEM),
         scratch_shapes=[
             pltpu.VMEM((2 * COLS * ROWS, 128), F32),
             pltpu.VMEM((BATCH, 2, 48, 128), F32),
             pltpu.VMEM((BATCH, 2, ROWS, 128), F32),
             pltpu.VMEM((COLS, 256), F32),
             pltpu.VMEM((COLS, 256), F32),
+            pltpu.VMEM((BINS, COLS, 256), BF),
+            pltpu.SemaphoreType.DMA((3,)),
         ],
         compiler_params=pltpu.CompilerParams(vmem_limit_bytes=40 << 20),
         name="microphysics",
@@ -541,10 +590,10 @@
 
 
 def coupling_kernel(
-    state, heat, echo, owner, heating, spread, slots,
+    state, heat, echo, sender, heating, spread, slots,
     tracer_next, power,
     field, packs, rows, got_packs, got_rows, sent, first_in, second_out, second_in,
-    send, recv, send1, recv1, send2, recv2,
+    send, recv, power_send, power_recv,
 ):
     g, c, up, down, left, right = neighbours()
     barrier = pltpu.get_barrier_semaphore()
@@ -553,6 +602,22 @@
     peers += [(r, s) for s in (left, right) for r in (up, down)]
     for to in peers:
         pl.semaphore_signal(barrier, inc=1, device_id=to, device_id_type=MESH)
+
+    sums = echo[...]
+    sums = jnp.concatenate([sums, pltpu.roll(sums, 16, 1)], axis=0)
+    sent[...] = dot_exact(sender[...], sums).reshape(NC, NG, 128)
+    pl.semaphore_wait(barrier, len(peers))
+    for k in range(1, NC):
+        to = lax.rem(c + k, NC)
+        pltpu.make_async_remote_copy(
+            src_ref=sent.at[to],
+            dst_ref=first_in.at[c],
+            send_sem=power_send.at[0],
+            recv_sem=power_recv.at[0],
+            device_id=(g, to),
+            device_id_type=MESH,
+        ).start()
+    first_in[c] = sent[c]
 
     warm = []
     for e in range(2):
@@ -564,86 +629,36 @@
         back = jnp.dot(heating[...], warm[:, at], preferred_element_type=F32)
         field[half * PTS : (half + 1) * PTS, :] = back + state[:, :, at].reshape(PTS, 128)
     pack_edges(field, packs, rows)
-    pl.semaphore_wait(barrier, len(peers))
-    copies = halo_copies(packs, rows, got_packs, got_rows, send, recv)
-    for copy in copies:
+    for copy in halo_copies(packs, rows, got_packs, got_rows, send, recv):
         copy.start()
 
-    across = jnp.broadcast_to(owner[...], (COLS, COLS))
-    i0 = lax.broadcasted_iota(jnp.int32, (COLS, COLS), 0)
-    i1 = lax.broadcasted_iota(jnp.int32, (COLS, COLS), 1)
-    along = jnp.sum(jnp.where(i0 == i1, across.astype(F32), 0.0), axis=1, keepdims=True)
-    earlier = (along == across.astype(F32)) & (i0 < i1)
-    turn = jnp.sum(jnp.where(earlier, 1.0, 0.0), axis=0, keepdims=True)
-    key = across % NC * NG + across // NC
-    onehot = jnp.concatenate(
-        [jnp.where((key == i0) & (turn == float(r)), 1.0, 0.0) for r in range(2)], axis=1
-    ).astype(BF)
-    sums = echo[...]
-    sums = jnp.concatenate([sums, pltpu.roll(sums, 16, 1)], axis=0)
-    sent[...] = dot_exact(onehot, sums).reshape(NC, NG, 128)
-    first = []
-    for k in range(1, NC):
-        to = lax.rem(c + k, NC)
-        copy = pltpu.make_async_remote_copy(
-            src_ref=sent.at[to],
-            dst_ref=first_in.at[c],
-            send_sem=send1.at[k],
-            recv_sem=recv1.at[c],
-            device_id=(g, to),
-            device_id_type=MESH,
-        )
-        copy.start()
-        first.append(copy)
-    first_in[c] = sent[c]
-
-    for copy in copies:
-        copy.wait()
-
-    def last(i, half, mean):
-        tracer_next[pl.ds(i * 8, 8), :, half * 128 : (half + 1) * 128] = mean
-
-    assemble_loop(field, got_packs, got_rows, last)
-
-    for k, copy in enumerate(first, 1):
-        copy.wait_send()
-        source = lax.rem(c + k, NC)
-        pltpu.make_async_remote_copy(
-            src_ref=sent.at[source],
-            dst_ref=first_in.at[source],
-            send_sem=send1.at[k],
-            recv_sem=recv1.at[source],
-            device_id=(g, source),
-            device_id_type=MESH,
-        ).wait_recv()
+    for sems in (power_recv, power_send):
+        wait_bytes(first_in.at[0 : NC - 1], sems.at[0])
     every = first_in[...]
     for to in range(NG):
         second_out[to] = every[:, to, :]
-    second = []
     for k in range(1, NG):
         to = lax.rem(g + k, NG)
-        copy = pltpu.make_async_remote_copy(
+        pltpu.make_async_remote_copy(
             src_ref=second_out.at[to],
             dst_ref=second_in.at[g],
-            send_sem=send2.at[k],
-            recv_sem=recv2.at[g],
+            send_sem=power_send.at[1],
+            recv_sem=power_recv.at[1],
             device_id=(to, c),
             device_id_type=MESH,
-        )
-        copy.start()
-        second.append(copy)
+        ).start()
     second_in[g] = second_out[g]
-    for k, copy in enumerate(second, 1):
-        copy.wait_send()
-        source = lax.rem(g + k, NG)
-        pltpu.make_async_remote_copy(
-            src_ref=second_out.at[source],
-            dst_ref=second_in.at[source],
-            send_sem=send2.at[k],
-            recv_sem=recv2.at[source],
-            device_id=(source, c),
-            device_id_type=MESH,
-        ).wait_recv()
+
+    halo_wait(got_packs, got_rows, send, recv)
+
+    def last(i, means):
+        for half in range(2):
+            tracer_next[pl.ds(i * 8, 8), :, half * 128 : (half + 1) * 128] = means[half].reshape(8, 8, 128)
+
+    assemble_loop(field, got_packs, got_rows, last)
+
+    for sems in (power_recv, power_send):
+        wait_bytes(second_in.at[0 : NG - 1], sems.at[1])
     turned = second_in[...].reshape(COLS, 128).T
     turned = jnp.concatenate([turned[0:16], turned[16:32]], axis=1)
     acc = None
@@ -653,7 +668,7 @@
     power[...] = acc
 
 
-def coupling(state, heat, echo, owner_row):
+def coupling(state, heat, echo, sender):
     return pl.pallas_call(
         coupling_kernel,
         out_shape=(
@@ -672,32 +687,30 @@
             pltpu.VMEM((NC, NG, 128), F32),
             pltpu.VMEM((NG, NC, 128), F32),
             pltpu.VMEM((NG, NC, 128), F32),
-            pltpu.SemaphoreType.DMA((8,)),
-            pltpu.SemaphoreType.DMA((8,)),
-            pltpu.SemaphoreType.DMA((NC,)),
-            pltpu.SemaphoreType.DMA((NC,)),
-            pltpu.SemaphoreType.DMA((NG,)),
-            pltpu.SemaphoreType.DMA((NG,)),
+            pltpu.SemaphoreType.DMA((2,)),
+            pltpu.SemaphoreType.DMA((2,)),
+            pltpu.SemaphoreType.DMA((2,)),
+            pltpu.SemaphoreType.DMA((2,)),
         ],
         compiler_params=pltpu.CompilerParams(
             collective_id=1, has_side_effects=True, vmem_limit_bytes=40 << 20
         ),
         name="coupling",
     )(
-        state, heat, echo, owner_row,
+        state, heat, echo, sender,
         jnp.asarray(heating_table()), jnp.asarray(spread_columns()), jnp.asarray(slot_table()),
     )
 
 
 def shards(tracer, wind_x, wind_y, drops, owner, counts, collision, growth):
-    state, cell_forcing, pair_coef, growth_col, start, sorted_counts, unsort = dynamics(
+    state, cell_forcing, pair_coef, growth_col, start, sorted_counts, unsort, sender = dynamics(
         tracer, wind_x, wind_y, drops.transpose(1, 0, 2),
-        counts.reshape(1, COLS), growth.reshape(1, BINS), collision,
+        counts.reshape(1, COLS), growth.reshape(1, BINS), collision, owner.reshape(1, COLS),
     )
     drops_next, heat, echo = microphysics(
         sorted_counts, start, cell_forcing, pair_coef, growth_col, unsort
     )
-    tracer_next, power = coupling(state, heat, echo, owner.reshape(1, COLS))
+    tracer_next, power = coupling(state, heat, echo, sender)
     return (tracer_next, drops_next.transpose(1, 0, 2), power)
 
 

time: 77.8 us -> 74.3 us (0.955); the launches traced: 76.6 us -> 74.2 us
  Pallas kernels: 74.5 us -> 72.1 us
    pallas_call x1, Pallas kernels: 40.2 us -> 11.6 us  [coupling(): pl.pallas_call(coupling_kernel, out_shape=(jax.ShapeDtypeStruct(state.sha...]
    pallas_call x1, Pallas kernels: 9.89 us -> 36.3 us  [microphysics(): pl.pallas_call(micro_kernel, out_shape=(jax.ShapeDtypeStruct((BINS, COLS,...]
where the time goes in v4:
time: 74.3 us; the launch traced here: 74.2 us
  Pallas kernels  72.1 us (97%)
  local copies, waits for them, and re-layouts  1.45 us (2%)
    pallas_call x1, Pallas kernels, microphysics(): pl.pallas_call(micro_kernel, out_shape=(jax.ShapeDtypeStruct((BINS, COLS,...  36.3 us
    pallas_call x1, Pallas kernels, dynamics(): pl.pallas_call(dynamics_kernel, out_shape=(jax.ShapeDtypeStruct(shape, F3...  24.2 us
    pallas_call x1, Pallas kernels, coupling(): pl.pallas_call(coupling_kernel, out_shape=(jax.ShapeDtypeStruct(state.sha...  11.6 us

profile of v4, /device:TPU:0, one launch (start us, length us, event | category | flops | bytes accessed | tf_op | source)
XLA Modules:
  0.0 74.2 jit_solution(11657846788907880020)
XLA Ops:
  0.6 0.0 copy-start.2
  0.6 24.2 %dynamics.1 = (f32[72,8,256]{2,1,0:T(8,128)S(1)}, f32[128,256]{1,0:T(8,128)S(1)}, bf16[48,576]{1,0:T(8,128)(2,1)S(1)}, f32[40,128]{1,0:T(8,128)S(1)}, f32[10240,...) custom-call(f32[72,8,256]{2,1,0:T(8,128)} %tracer_h.1, ...), custom_call_target="tpu_custom_call" | custom-call | tf_op jit(solution)/shard_map/dynamics/pallas_call | solution.py:439
  24.9 0.0 copy-done.2
  24.9 0.0 copy-start
  24.9 0.0 copy-start.1
  24.9 0.0 copy-start.3
  24.9 36.3 %microphysics.1 = (bf16[33,128,256]{2,1,0:T(8,128)(2,1)}, bf16[128,128]{1,0:T(8,128)(2,1)S(1)}, f32[128,128]{1,0:T(8,128)S(1)}) custom-call(s32[1,128]{1,0:T(1,128)S(1)} %get-tuple-element.17.counts, f32[10240,128]{1,0:T(8,128)S(1)} %get-tuple-element.18.start, f32[128,256]{1,0:T(8,128)S(1)} %get-tuple-element.19.cell_forcing, ...), custom_call_target="tpu_custom_call" | custom-call | tf_op jit(solution)/shard_map/microphysics/pallas_call | solution.py:569
  61.2 0.0 copy-done
  61.2 0.0 copy-done.1
  61.2 0.0 copy-done.3
  61.2 11.6 %coupling.1 = (f32[72,8,256]{2,1,0:T(8,128)S(1)}, f32[16,256]{1,0:T(8,128)S(1)}) custom-call(f32[72,8,256]{2,1,0:T(8,128)S(1)} %get-tuple-element.16.state, bf16[128,128]{1,0:T(8,128)(2,1)S(1)} %get-tuple-element.23.heat, f32[128,128]{1,0:T(8,128)S(1)} %get-tuple-element.24.echo, bf16[128,256]{1,0:T(8,128)(2,1)S(1)} %get-tuple-element.25.sender, ...), custom_call_target="tpu_custom_call" | custom-call | tf_op jit(solution)/shard_map/coupling/pallas_call | solution.py:672
  72.8 0.8 %copy.23 = f32[72,8,256]{2,1,0:T(8,128)} copy(f32[72,8,256]{2,1,0:T(8,128)S(1)} %get-tuple-element.32) | data formatting | bytes 1179648
  73.6 0.6 copy.24
Async XLA Ops:
  0.6 24.2 %copy-start.2 = (bf16[256,128]{1,0:T(8,128)(2,1)S(1)}, bf16[256,128]{1,0:T(8,128)(2,1)}, u32[]{:S(2)}) copy-start(bf16[256,128]{1,0:T(8,128)(2,1)} %constant.26.clone.group) | copy-start | bytes 196612
  24.9 36.3 %copy-start = (bf16[576,64]{1,0:T(8,128)(2,1)S(1)}, bf16[576,64]{1,0:T(8,128)(2,1)}, u32[]{:S(2)}) copy-start(bf16[576,64]{1,0:T(8,128)(2,1)} %constant.27.clone.heating) | copy-start | bytes 221188
  24.9 36.3 %copy-start.1 = (bf16[256,256]{1,0:T(8,128)(2,1)S(1)}, bf16[256,256]{1,0:T(8,128)(2,1)}, u32[]{:S(2)}) copy-start(bf16[256,256]{1,0:T(8,128)(2,1)} %constant.29.clone.slots) | copy-start | bytes 393220
  24.9 36.3 %copy-start.3 = (bf16[64,256]{1,0:T(8,128)(2,1)S(1)}, bf16[64,256]{1,0:T(8,128)(2,1)}, u32[]{:S(2)}) copy-start(bf16[64,256]{1,0:T(8,128)(2,1)} %constant.28.clone.spread) | copy-start | bytes 98308

commit v5 on v4

--- a/solution.py
+++ b/solution.py
@@ -30,6 +30,7 @@
 DT_PHYS = 0.5
 BATCH = 32
 ROWS = 40
+EARLY = 3
 
 
 def gll_tables():
@@ -144,6 +145,14 @@
     return out.astype(ml_dtypes.bfloat16)
 
 
+def pair_members():
+    out = np.zeros((2, PAIRS, 128), np.float32)
+    for q, pair in enumerate(pair_list()):
+        for side in range(2):
+            out[side, q, pair[side]] = 1.0
+    return out.astype(ml_dtypes.bfloat16)
+
+
 def split3(x):
     hi = x.astype(BF)
     rest = x - hi.astype(F32)
@@ -169,6 +178,27 @@
         y = jnp.dot(both, by_cols, preferred_element_type=F32)
         grad_y.append(y[:, 0:128] + y[:, 128:256])
     return wind_x * grad_x + wind_y * jnp.concatenate(grad_y, axis=1)
+
+
+def pairs_of(now, doubled):
+    doubled[0:32, :] = now[0:32]
+    doubled[32:48, :] = now[0:16]
+    near, far = [], []
+    for d in range(8):
+        shifted = doubled[d : d + 40, :]
+        near.append((now[0:32] * shifted[0:32]).astype(BF))
+        far.append((now[0:32] * shifted[8:40]).astype(BF))
+    last = jnp.broadcast_to(now[32:33], (32, 128))
+    rest = [
+        (now[0:16] * now[16:32]).astype(BF),
+        (now[0:32] * last).astype(BF),
+        (last[0:16] * last[0:16]).astype(BF),
+    ]
+    return jnp.concatenate(near + far + rest, axis=0)
+
+
+def column_rows(col, half):
+    return pl.ds(pl.multiple_of((half * COLS + col) * ROWS, 8), ROWS)
 
 
 def neighbours():
@@ -296,10 +326,10 @@
 
 def dynamics_kernel(
     tracer_h, wind_x_h, wind_y_h, drops_h, counts_h, growth_h, collision_h, by_rows_h, by_cols_h, selector_h,
-    row_map_h, col_map_h, cells_h, owner_h,
-    state, cell_forcing, pair_coef, growth_col, start, counts_out, unsort, sender,
+    row_map_h, col_map_h, cells_h, owner_h, members_h,
+    state, cell_forcing, pair_coef, growth_col, start, counts_out, unsort, sender, quadratic, linear, constant,
     tracer, wind_x, wind_y, drops, counts, growth, collision, by_rows, by_cols, selector,
-    row_map, col_map, cells, owner,
+    row_map, col_map, cells, owner, members, doubled,
     loads, field, total, packs, rows, got_packs, got_rows, send, recv,
 ):
     g, c, up, down, left, right = neighbours()
@@ -307,9 +337,9 @@
     around = [(up, c), (down, c)]
     around += [(r, s) for s in (left, right) for r in (g, up, down)]
     sources = [tracer_h, by_rows_h, by_cols_h, wind_x_h, wind_y_h, drops_h, counts_h, owner_h, collision_h,
-               selector_h, growth_h, row_map_h, col_map_h, cells_h]
+               selector_h, growth_h, members_h, row_map_h, col_map_h, cells_h]
     targets = [tracer, by_rows, by_cols, wind_x, wind_y, drops, counts, owner, collision,
-               selector, growth, row_map, col_map, cells]
+               selector, growth, members, row_map, col_map, cells]
     fetch = [
         pltpu.make_async_copy(source, target, loads.at[n])
         for n, (source, target) in enumerate(zip(sources, targets))
@@ -341,10 +371,9 @@
 
     for copy in fetch[5:]:
         copy.wait()
-    pair_coef[0:33, :] = jnp.dot(
-        collision[...], selector[...], preferred_element_type=F32
-    ).astype(BF)
-    pair_coef[33:48, :] = jnp.zeros((15, PAIRS), BF)
+    coef = jnp.dot(collision[...], selector[...], preferred_element_type=F32)
+    coef = jnp.concatenate([coef, jnp.zeros((15, PAIRS), F32)], axis=0)
+    pair_coef[...] = coef.astype(BF)
     i0 = lax.broadcasted_iota(jnp.int32, (COLS, COLS), 0)
     i1 = lax.broadcasted_iota(jnp.int32, (COLS, COLS), 1)
     wide = jnp.concatenate([growth[...], jnp.zeros((1, COLS - BINS), F32)], axis=1)
@@ -354,6 +383,22 @@
         ),
         (ROWS, COLS),
     )
+    stacked = jnp.concatenate([jnp.broadcast_to(x.astype(F32), (16, COLS)) for x in split3(wide)], axis=0)
+    slope = jnp.zeros((96, COLS), F32)
+    for side in range(2):
+        of_pair = lax.dot_general(
+            stacked.astype(BF), members[side], (((1,), (1,)), ((), ())), preferred_element_type=F32
+        )
+        scaled = coef * (of_pair[0:1] + of_pair[16:17] + of_pair[32:33])
+        near = scaled.astype(BF)
+        terms = jnp.concatenate([near, (scaled - near.astype(F32)).astype(BF)], axis=0)
+        slope = slope + jnp.dot(terms, members[1 - side], preferred_element_type=F32)
+    slope = slope[0:48] + slope[48:96]
+    constant[...] = jnp.broadcast_to(
+        0.5 * jnp.sum(slope[0:ROWS] * wide, axis=1, keepdims=True), (ROWS, COLS)
+    )
+    near = slope.astype(BF)
+    linear[...] = jnp.concatenate([near, (slope - near.astype(F32)).astype(BF)], axis=0)
     across = jnp.broadcast_to(counts[...], (COLS, COLS)).astype(F32)
     along = jnp.sum(jnp.where(i0 == i1, across, 0.0), axis=1, keepdims=True)
     before = (across > along) | ((across == along) & (i1 < i0))
@@ -382,6 +427,17 @@
         [jnp.where((key == i0) & (turn == float(r)), 1.0, 0.0) for r in range(2)], axis=1
     ).astype(BF)
 
+    def square(p, _):
+        for b in range(16):
+            blocks = [
+                pairs_of(start[column_rows(p * 16 + b, half), :], doubled.at[b, half]) for half in range(2)
+            ]
+            found = jnp.dot(pair_coef[...], jnp.concatenate(blocks, axis=1), preferred_element_type=F32)
+            for half in range(2):
+                quadratic[column_rows(p * 16 + b, half), :] = found[0:ROWS, half * 128 : (half + 1) * 128]
+        return 0
+
+    lax.fori_loop(0, EARLY, square, 0)
     halo_wait(got_packs.at[0], got_rows.at[0], send.at[0], recv.at[0])
 
     def second(i, means):
@@ -399,6 +455,7 @@
     copies = halo_copies(packs.at[1], rows.at[1], got_packs.at[1], got_rows.at[1], send.at[1], recv.at[1])
     for copy in copies:
         copy.start()
+    lax.fori_loop(EARLY, COLS // 16, square, 0)
     halo_wait(got_packs.at[1], got_rows.at[1], send.at[1], recv.at[1])
 
     def third(i, means):
@@ -435,6 +492,7 @@
         tracer, wind_x, wind_y, drops, counts_row, growth_row, collision,
         jnp.asarray(by_rows), jnp.asarray(by_cols), jnp.asarray(pair_selector()),
         jnp.asarray(row_map), jnp.asarray(col_map), jnp.asarray(spread_cells()), owner_row,
+        jnp.asarray(pair_members()),
     )
     return pl.pallas_call(
         dynamics_kernel,
@@ -447,12 +505,16 @@
             jax.ShapeDtypeStruct((1, COLS), jnp.int32),
             jax.ShapeDtypeStruct((COLS, COLS), BF),
             jax.ShapeDtypeStruct((COLS, 2 * COLS), BF),
+            jax.ShapeDtypeStruct((2 * COLS * ROWS, 128), F32),
+            jax.ShapeDtypeStruct((96, 128), BF),
+            jax.ShapeDtypeStruct((ROWS, 128), F32),
         ),
-        in_specs=[HBM] * 14,
-        out_specs=(VMEM,) * 8,
+        in_specs=[HBM] * 15,
+        out_specs=(VMEM,) * 11,
         scratch_shapes=[pltpu.VMEM(x.shape, x.dtype) for x in operands]
         + [
-            pltpu.SemaphoreType.DMA((14,)),
+            pltpu.VMEM((16, 2, 48, 128), F32),
+            pltpu.SemaphoreType.DMA((15,)),
             pltpu.VMEM((2 * PTS, 128), F32),
             pltpu.VMEM((2 * PTS, 128), F32),
             pltpu.VMEM((2, 2, 8, 128), F32),
@@ -470,7 +532,7 @@
 
 
 def micro_kernel(
-    counts, start, cell_forcing, pair_coef, growth, group, unsort,
+    counts, start, cell_forcing, pair_coef, growth, group, unsort, quadratic, linear, constant,
     drops_next, heat_out, echo_out,
     cloud, doubled, grow, heat_rows, echo_rows, drops_out, stores,
 ):
@@ -479,31 +541,14 @@
     srow = lax.broadcasted_iota(jnp.int32, (8, 128), 0)
 
     def place(p, b, half):
-        return pl.ds(pl.multiple_of((half * COLS + p * BATCH + b) * ROWS, 8), ROWS)
+        return column_rows(p * BATCH + b, half)
 
     def substep(s, p):
         for b in range(BATCH):
             active = s < counts[0, p * BATCH + b]
-            blocks, grown, olds = [], [], []
-            for half in range(2):
-                old = cloud[place(p, b, half), :]
-                now = old + grow[b, half]
-                doubled[b, half, 0:32, :] = now[0:32]
-                doubled[b, half, 32:48, :] = now[0:16]
-                near, far = [], []
-                for d in range(8):
-                    shifted = doubled[b, half, d : d + 40, :]
-                    near.append((now[0:32] * shifted[0:32]).astype(BF))
-                    far.append((now[0:32] * shifted[8:40]).astype(BF))
-                last = jnp.broadcast_to(now[32:33], (32, 128))
-                rest = [
-                    (now[0:16] * now[16:32]).astype(BF),
-                    (now[0:32] * last).astype(BF),
-                    (last[0:16] * last[0:16]).astype(BF),
-                ]
-                blocks.append(jnp.concatenate(near + far + rest, axis=0))
-                grown.append(now)
-                olds.append(old)
+            olds = [cloud[place(p, b, half), :] for half in range(2)]
+            grown = [olds[half] + grow[b, half] for half in range(2)]
+            blocks = [pairs_of(grown[half], doubled.at[b, half]) for half in range(2)]
             change = jnp.dot(
                 pair_coef[...], jnp.concatenate(blocks, axis=1), preferred_element_type=F32
             )
@@ -514,11 +559,22 @@
 
     def batch(p, _):
         for b in range(BATCH):
+            active = counts[0, p * BATCH + b] > 0
             forced = cell_forcing[pl.ds(p * BATCH + b, 1), :]
+            olds = [start[place(p, b, half), :] for half in range(2)]
+            rows = [jnp.concatenate([old, old[0:8]], axis=0).astype(BF) for old in olds]
+            sloped = jnp.dot(linear[:, 0:48], jnp.concatenate(rows, axis=1), preferred_element_type=F32)
             for half in range(2):
-                cloud[place(p, b, half), :] = start[place(p, b, half), :]
-                grow[b, half] = forced[:, half * 128 : (half + 1) * 128] * growth[...]
-        lax.fori_loop(0, counts[0, p * BATCH], substep, p)
+                at = slice(half * 128, (half + 1) * 128)
+                f = forced[:, at]
+                add = f * growth[...]
+                change = quadratic[place(p, b, half), :] + f * (
+                    sloped[0:ROWS, at] + sloped[48 : 48 + ROWS, at] + f * constant[...]
+                )
+                grow[b, half] = add
+                moved = olds[half] + add + DT_CRM * change
+                cloud[place(p, b, half), :] = jnp.where(active, moved, olds[half])
+        lax.fori_loop(1, counts[0, p * BATCH], substep, p)
         for half in range(2):
             at = slice(half * 128, (half + 1) * 128)
             for eight in range(BATCH // 8):
@@ -565,7 +621,7 @@
         piece.wait()
 
 
-def microphysics(counts, start, cell_forcing, pair_coef, growth, unsort):
+def microphysics(counts, start, cell_forcing, pair_coef, growth, unsort, quadratic, linear, constant):
     return pl.pallas_call(
         micro_kernel,
         out_shape=(
@@ -573,7 +629,7 @@
             jax.ShapeDtypeStruct((COLS, 128), BF),
             jax.ShapeDtypeStruct((COLS, 128), F32),
         ),
-        in_specs=[SMEM] + [VMEM] * 6,
+        in_specs=[SMEM] + [VMEM] * 9,
         out_specs=(HBM, VMEM, VMEM),
         scratch_shapes=[
             pltpu.VMEM((2 * COLS * ROWS, 128), F32),
@@ -586,7 +642,10 @@
         ],
         compiler_params=pltpu.CompilerParams(vmem_limit_bytes=40 << 20),
         name="microphysics",
-    )(counts, start, cell_forcing, pair_coef, growth, jnp.asarray(group_matrix()), unsort)
+    )(
+        counts, start, cell_forcing, pair_coef, growth, jnp.asarray(group_matrix()), unsort,
+        quadratic, linear, constant,
+    )
 
 
 def coupling_kernel(
@@ -703,12 +762,12 @@
 
 
 def shards(tracer, wind_x, wind_y, drops, owner, counts, collision, growth):
-    state, cell_forcing, pair_coef, growth_col, start, sorted_counts, unsort, sender = dynamics(
+    state, cell_forcing, pair_coef, growth_col, start, sorted_counts, unsort, sender, quadratic, linear, constant = dynamics(
         tracer, wind_x, wind_y, drops.transpose(1, 0, 2),
         counts.reshape(1, COLS), growth.reshape(1, BINS), collision, owner.reshape(1, COLS),
     )
     drops_next, heat, echo = microphysics(
-        sorted_counts, start, cell_forcing, pair_coef, growth_col, unsort
+        sorted_counts, start, cell_forcing, pair_coef, growth_col, unsort, quadratic, linear, constant
     )
     tracer_next, power = coupling(state, heat, echo, sender)
     return (tracer_next, drops_next.transpose(1, 0, 2), power)

time: 74.3 us -> 67 us (0.902); the launches traced: 74.2 us -> 65.8 us
  Pallas kernels: 72.1 us -> 63.7 us
    pallas_call x1, Pallas kernels: 36.3 us -> 6.78 us  [microphysics(): pl.pallas_call(micro_kernel, out_shape=(jax.ShapeDtypeStruct((BINS, COLS,...]
    pallas_call x1, Pallas kernels: 11.6 us -> 32.6 us  [coupling(): pl.pallas_call(coupling_kernel, out_shape=(jax.ShapeDtypeStruct(state.sha...]
where the time goes in v5:
time: 67 us; the launch traced here: 65.8 us
  Pallas kernels  63.7 us (95%)
  local copies, waits for them, and re-layouts  1.45 us (2%)
  between operations  0.72 us (1%)
    pallas_call x1, Pallas kernels, coupling(): pl.pallas_call(coupling_kernel, out_shape=(jax.ShapeDtypeStruct(state.sha...  32.6 us
    pallas_call x1, Pallas kernels, dynamics(): pl.pallas_call(dynamics_kernel, out_shape=(jax.ShapeDtypeStruct(shape, F3...  24.3 us
    pallas_call x1, Pallas kernels, microphysics(): pl.pallas_call(micro_kernel, out_shape=(jax.ShapeDtypeStruct((BINS, COLS,...  6.78 us
    unnamed x10, local copies, waits for them, and re-layouts  1.45 us

profile of v5, /device:TPU:0, one launch (start us, length us, event | category | flops | bytes accessed | tf_op | source)
XLA Modules:
  0.0 65.8 jit_solution(7979011187418455860)
XLA Ops:
  0.6 0.0 copy-start.2
  0.6 24.3 %dynamics.1 = (f32[72,8,256]{2,1,0:T(8,128)S(1)}, f32[128,256]{1,0:T(8,128)S(1)}, bf16[48,576]{1,0:T(8,128)(2,1)S(1)}, f32[40,128]{1,0:T(8,128)S(1)}, f32[10240,...) custom-call(f32[72,8,256]{2,1,0:T(8,128)} %tracer_h.1, ...), custom_call_target="tpu_custom_call" | custom-call | tf_op jit(solution)/shard_map/dynamics/pallas_call | solution.py:497
  25.0 0.0 copy-done.2
  25.0 0.0 copy-start
  25.0 0.0 copy-start.1
  25.0 0.0 copy-start.3
  25.0 6.8 %microphysics.1 = (bf16[33,128,256]{2,1,0:T(8,128)(2,1)}, bf16[128,128]{1,0:T(8,128)(2,1)S(1)}, f32[128,128]{1,0:T(8,128)S(1)}) custom-call(s32[1,128]{1,0:T(1,128)S(1)} %get-tuple-element.20.counts, f32[10240,128]{1,0:T(8,128)S(1)} %get-tuple-element.21.start, f32[128,256]{1,0:T(8,128)S(1)} %get-tuple-element.22.cell_forcing, ...), custom_call_target="tpu_custom_call" | custom-call | tf_op jit(solution)/shard_map/microphysics/pallas_call | solution.py:625
  31.8 0.0 copy-done
  31.8 0.0 copy-done.1
  31.8 0.0 copy-done.3
  31.8 32.6 %coupling.1 = (f32[72,8,256]{2,1,0:T(8,128)S(1)}, f32[16,256]{1,0:T(8,128)S(1)}) custom-call(f32[72,8,256]{2,1,0:T(8,128)S(1)} %get-tuple-element.19.state, bf16[128,128]{1,0:T(8,128)(2,1)S(1)} %get-tuple-element.29.heat, f32[128,128]{1,0:T(8,128)S(1)} %get-tuple-element.30.echo, bf16[128,256]{1,0:T(8,128)(2,1)S(1)} %get-tuple-element.31.sender, ...), custom_call_target="tpu_custom_call" | custom-call | tf_op jit(solution)/shard_map/coupling/pallas_call | solution.py:731
  64.4 0.8 %copy.24 = f32[72,8,256]{2,1,0:T(8,128)} copy(f32[72,8,256]{2,1,0:T(8,128)S(1)} %get-tuple-element.38) | data formatting | bytes 1179648
  65.2 0.6 copy.25
Async XLA Ops:
  0.6 24.3 %copy-start.2 = (bf16[256,128]{1,0:T(8,128)(2,1)S(1)}, bf16[256,128]{1,0:T(8,128)(2,1)}, u32[]{:S(2)}) copy-start(bf16[256,128]{1,0:T(8,128)(2,1)} %constant.29.clone.group) | copy-start | bytes 196612
  25.0 6.8 %copy-start = (bf16[576,64]{1,0:T(8,128)(2,1)S(1)}, bf16[576,64]{1,0:T(8,128)(2,1)}, u32[]{:S(2)}) copy-start(bf16[576,64]{1,0:T(8,128)(2,1)} %constant.30.clone.heating) | copy-start | bytes 221188
  25.0 6.8 %copy-start.1 = (bf16[256,256]{1,0:T(8,128)(2,1)S(1)}, bf16[256,256]{1,0:T(8,128)(2,1)}, u32[]{:S(2)}) copy-start(bf16[256,256]{1,0:T(8,128)(2,1)} %constant.32.clone.slots) | copy-start | bytes 393220
  25.0 6.8 %copy-start.3 = (bf16[64,256]{1,0:T(8,128)(2,1)S(1)}, bf16[64,256]{1,0:T(8,128)(2,1)}, u32[]{:S(2)}) copy-start(bf16[64,256]{1,0:T(8,128)(2,1)} %constant.31.clone.spread) | copy-start | bytes 98308

commit v6 on v5

--- a/solution.py
+++ b/solution.py
@@ -30,7 +30,7 @@
 DT_PHYS = 0.5
 BATCH = 32
 ROWS = 40
-EARLY = 3
+EARLY = 1
 
 
 def gll_tables():
@@ -126,9 +126,10 @@
 
 def pair_list():
     out = []
-    for d in range(16):
-        for i in range(32):
-            out.append((i, (i + d) % 32))
+    for back in (0, 8):
+        for d in range(8):
+            for i in range(32):
+                out.append(((i - back) % 32, (i + d) % 32))
     for i in range(16):
         out.append((i, i + 16))
     for i in range(32):
@@ -180,21 +181,38 @@
     return wind_x * grad_x + wind_y * jnp.concatenate(grad_y, axis=1)
 
 
-def pairs_of(now, doubled):
-    doubled[0:32, :] = now[0:32]
-    doubled[32:48, :] = now[0:16]
-    near, far = [], []
-    for d in range(8):
-        shifted = doubled[d : d + 40, :]
-        near.append((now[0:32] * shifted[0:32]).astype(BF))
-        far.append((now[0:32] * shifted[8:40]).astype(BF))
-    last = jnp.broadcast_to(now[32:33], (32, 128))
-    rest = [
-        (now[0:16] * now[16:32]).astype(BF),
-        (now[0:32] * last).astype(BF),
-        (last[0:16] * last[0:16]).astype(BF),
-    ]
-    return jnp.concatenate(near + far + rest, axis=0)
+def pairs_of(grown, doubled):
+    for half in range(2):
+        doubled[half, 0:32, :] = grown[half][0:32]
+        doubled[half, 32:40, :] = grown[half][0:8]
+
+    def beside(parts):
+        return jnp.concatenate(parts, axis=1)
+
+    here = beside([now[0:32].astype(BF) for now in grown])
+    behind = beside([jnp.concatenate([now[24:32], now[0:24]], axis=0).astype(BF) for now in grown])
+    ahead = [beside([doubled[half, d : d + 32, :].astype(BF) for half in range(2)]) for d in range(8)]
+    last = beside([jnp.broadcast_to(now[32:33], (32, 128)).astype(BF) for now in grown])
+    rows = [here * x for x in ahead] + [behind * x for x in ahead]
+    rows += [here[0:16] * here[16:32], here * last, last[0:16] * last[0:16]]
+    return jnp.concatenate(rows, axis=0)
+
+
+def rows_of_sums(blocks):
+    row = lax.broadcasted_iota(jnp.int32, (8, 128), 0)
+    for step in (4, 2, 1):
+        mine = row % (2 * step) < step
+        merged = []
+        for k in range(step):
+            a, b = blocks[k], blocks[k + step]
+            other = jnp.where(mine, b, a)
+            if step == 4:
+                moved = pltpu.roll(other, 4, 0)
+            else:
+                moved = jnp.where(mine, pltpu.roll(other, 8 - step, 0), pltpu.roll(other, step, 0))
+            merged.append(jnp.where(mine, a, b) + moved)
+        blocks = merged
+    return blocks[0]
 
 
 def column_rows(col, half):
@@ -330,28 +348,36 @@
     state, cell_forcing, pair_coef, growth_col, start, counts_out, unsort, sender, quadratic, linear, constant,
     tracer, wind_x, wind_y, drops, counts, growth, collision, by_rows, by_cols, selector,
     row_map, col_map, cells, owner, members, doubled,
-    loads, field, total, packs, rows, got_packs, got_rows, send, recv,
+    loads, piece_loads, field, total, packs, rows, got_packs, got_rows, send, recv,
 ):
     g, c, up, down, left, right = neighbours()
     barrier = pltpu.get_barrier_semaphore()
     around = [(up, c), (down, c)]
     around += [(r, s) for s in (left, right) for r in (g, up, down)]
-    sources = [tracer_h, by_rows_h, by_cols_h, wind_x_h, wind_y_h, drops_h, counts_h, owner_h, collision_h,
+    sources = [tracer_h, wind_x_h, wind_y_h, by_rows_h, by_cols_h, drops_h, counts_h, owner_h, collision_h,
                selector_h, growth_h, members_h, row_map_h, col_map_h, cells_h]
-    targets = [tracer, by_rows, by_cols, wind_x, wind_y, drops, counts, owner, collision,
+    targets = [tracer, wind_x, wind_y, by_rows, by_cols, drops, counts, owner, collision,
                selector, growth, members, row_map, col_map, cells]
+    thirds = [
+        [
+            pltpu.make_async_copy(source.at[pl.ds(24 * n, 24)], target.at[pl.ds(24 * n, 24)], piece_loads.at[n, m])
+            for m, (source, target) in enumerate(zip(sources[0:3], targets[0:3]))
+        ]
+        for n in range(3)
+    ]
     fetch = [
         pltpu.make_async_copy(source, target, loads.at[n])
-        for n, (source, target) in enumerate(zip(sources, targets))
+        for n, (source, target) in enumerate(zip(sources[3:], targets[3:]))
     ]
-    for copy in fetch:
+    for copy in fetch[0:2] + thirds[0] + thirds[1] + thirds[2] + fetch[2:]:
         copy.start()
     for to in around:
         pl.semaphore_signal(barrier, inc=1, device_id=to, device_id_type=MESH)
-    for copy in fetch[0:5]:
+    for copy in fetch[0:2]:
         copy.wait()
-
-    def first(n, _):
+    for n in range(3):
+        for copy in thirds[n]:
+            copy.wait()
         for k in range(3):
             i = n * 3 + k
             put_halves(
@@ -360,16 +386,13 @@
                     chunk_of(tracer, i), chunk_of(wind_x, i), chunk_of(wind_y, i), by_rows[...], by_cols[...]
                 ),
             )
-        return 0
-
-    lax.fori_loop(0, 3, first, 0)
     pack_edges(field, packs.at[0], rows.at[0])
     pl.semaphore_wait(barrier, 8)
     copies = halo_copies(packs.at[0], rows.at[0], got_packs.at[0], got_rows.at[0], send.at[0], recv.at[0])
     for copy in copies:
         copy.start()
 
-    for copy in fetch[5:]:
+    for copy in fetch[2:]:
         copy.wait()
     coef = jnp.dot(collision[...], selector[...], preferred_element_type=F32)
     coef = jnp.concatenate([coef, jnp.zeros((15, PAIRS), F32)], axis=0)
@@ -429,10 +452,8 @@
 
     def square(p, _):
         for b in range(16):
-            blocks = [
-                pairs_of(start[column_rows(p * 16 + b, half), :], doubled.at[b, half]) for half in range(2)
-            ]
-            found = jnp.dot(pair_coef[...], jnp.concatenate(blocks, axis=1), preferred_element_type=F32)
+            drops_of = [start[column_rows(p * 16 + b, half), :] for half in range(2)]
+            found = jnp.dot(pair_coef[...], pairs_of(drops_of, doubled.at[b]), preferred_element_type=F32)
             for half in range(2):
                 quadratic[column_rows(p * 16 + b, half), :] = found[0:ROWS, half * 128 : (half + 1) * 128]
         return 0
@@ -466,11 +487,11 @@
             total[pl.ds(at, 64), :] = total[pl.ds(at, 64), :] + means[half]
 
     assemble_loop(field, got_packs.at[1], got_rows.at[1], third)
-    parts = [
-        jnp.dot(row_map[...], total[half * PTS : (half + 1) * PTS, :], precision=HIGH, preferred_element_type=F32)
-        for half in range(2)
-    ]
-    by_row = jnp.concatenate(parts, axis=1)
+    sums = jnp.concatenate([total[0:PTS, :], total[PTS : 2 * PTS, :]], axis=1)
+    near = sums.astype(BF)
+    rest = (sums - near.astype(F32)).astype(BF)
+    by_row = jnp.dot(row_map[...], near, preferred_element_type=F32)
+    by_row = by_row[0:32] + by_row[32:64] + jnp.dot(row_map[0:32, :], rest, preferred_element_type=F32)
     forcing = [
         lax.dot_general(
             col_map[...], by_row[16 * e : 16 * (e + 1)], (((1,), (1,)), ((), ())),
@@ -486,6 +507,8 @@
 
 def dynamics(tracer, wind_x, wind_y, drops, counts_row, growth_row, collision, owner_row):
     row_map, col_map = forcing_tables()
+    near = row_map.astype(ml_dtypes.bfloat16)
+    row_map = np.concatenate([near, (row_map - near.astype(np.float32)).astype(ml_dtypes.bfloat16)])
     by_rows, by_cols = stencil_tables()
     shape = tracer.shape
     operands = (
@@ -514,7 +537,8 @@
         scratch_shapes=[pltpu.VMEM(x.shape, x.dtype) for x in operands]
         + [
             pltpu.VMEM((16, 2, 48, 128), F32),
-            pltpu.SemaphoreType.DMA((15,)),
+            pltpu.SemaphoreType.DMA((12,)),
+            pltpu.SemaphoreType.DMA((3, 3)),
             pltpu.VMEM((2 * PTS, 128), F32),
             pltpu.VMEM((2 * PTS, 128), F32),
             pltpu.VMEM((2, 2, 8, 128), F32),
@@ -538,7 +562,6 @@
 ):
     bins = lax.broadcasted_iota(jnp.int32, (ROWS, 128), 0)
     mass = jnp.where(bins < BINS, (bins.astype(F32) + 1.0) / BINS, 0.0)
-    srow = lax.broadcasted_iota(jnp.int32, (8, 128), 0)
 
     def place(p, b, half):
         return column_rows(p * BATCH + b, half)
@@ -548,10 +571,7 @@
             active = s < counts[0, p * BATCH + b]
             olds = [cloud[place(p, b, half), :] for half in range(2)]
             grown = [olds[half] + grow[b, half] for half in range(2)]
-            blocks = [pairs_of(grown[half], doubled.at[b, half]) for half in range(2)]
-            change = jnp.dot(
-                pair_coef[...], jnp.concatenate(blocks, axis=1), preferred_element_type=F32
-            )
+            change = jnp.dot(pair_coef[...], pairs_of(grown, doubled.at[b]), preferred_element_type=F32)
             for half in range(2):
                 moved = grown[half] + DT_CRM * change[0:ROWS, half * 128 : (half + 1) * 128]
                 cloud[place(p, b, half), :] = jnp.where(active, moved, olds[half])
@@ -578,16 +598,16 @@
         for half in range(2):
             at = slice(half * 128, (half + 1) * 128)
             for eight in range(BATCH // 8):
-                heats = jnp.zeros((8, 128), F32)
-                echos = jnp.zeros((8, 128), F32)
+                heats, echos = [], []
                 for b in range(8):
                     where = place(p, eight * 8 + b, half)
                     final = cloud[where, :]
                     gain = (final - start[where, :]) * mass
                     weighed = final * mass
                     square = weighed * weighed
-                    heats = jnp.where(srow == b, jnp.sum(gain, axis=0, keepdims=True), heats)
-                    echos = jnp.where(srow == b, jnp.sum(square, axis=0, keepdims=True), echos)
+                    heats.append(sum(gain[8 * k : 8 * k + 8] for k in range(5)))
+                    echos.append(sum(square[8 * k : 8 * k + 8] for k in range(5)))
+                heats, echos = rows_of_sums(heats), rows_of_sums(echos)
                 rows = pl.ds(pl.multiple_of(p * BATCH + eight * 8, 8), 8)
                 heat_rows[rows, at] = heats
                 echo_rows[rows, at] = echos
@@ -649,8 +669,8 @@
 
 
 def coupling_kernel(
-    state, heat, echo, sender, heating, spread, slots,
-    tracer_next, power,
+    state, heat, echo, sender, heating, spread,
+    tracer_next, rows_out,
     field, packs, rows, got_packs, got_rows, sent, first_in, second_out, second_in,
     send, recv, power_send, power_recv,
 ):
@@ -718,13 +738,7 @@
 
     for sems in (power_recv, power_send):
         wait_bytes(second_in.at[0 : NG - 1], sems.at[1])
-    turned = second_in[...].reshape(COLS, 128).T
-    turned = jnp.concatenate([turned[0:16], turned[16:32]], axis=1)
-    acc = None
-    for part in split3(turned):
-        y = jnp.dot(part, slots[...], preferred_element_type=F32)
-        acc = y if acc is None else acc + y
-    power[...] = acc
+    rows_out[...] = second_in[...].reshape(COLS, 128)
 
 
 def coupling(state, heat, echo, sender):
@@ -732,9 +746,9 @@
         coupling_kernel,
         out_shape=(
             jax.ShapeDtypeStruct(state.shape, F32),
-            jax.ShapeDtypeStruct((CLEV, 256), F32),
+            jax.ShapeDtypeStruct((COLS, 128), F32),
         ),
-        in_specs=[VMEM] * 7,
+        in_specs=[VMEM] * 6,
         out_specs=(VMEM,) * 2,
         scratch_shapes=[
             pltpu.VMEM((2 * PTS, 128), F32),
@@ -757,8 +771,33 @@
         name="coupling",
     )(
         state, heat, echo, sender,
-        jnp.asarray(heating_table()), jnp.asarray(spread_columns()), jnp.asarray(slot_table()),
+        jnp.asarray(heating_table()), jnp.asarray(spread_columns()),
     )
+
+
+def finish_kernel(mean, rows, slots, tracer_next, power, store):
+    copy = pltpu.make_async_copy(mean, tracer_next, store)
+    copy.start()
+    turned = rows[...].T
+    turned = jnp.concatenate([turned[0:16], turned[16:32]], axis=1)
+    parts = jnp.dot(jnp.concatenate(split3(turned), axis=0), slots[...], preferred_element_type=F32)
+    power[...] = parts[0:16] + parts[16:32] + parts[32:48]
+    copy.wait()
+
+
+def finish(mean, rows):
+    return pl.pallas_call(
+        finish_kernel,
+        out_shape=(
+            jax.ShapeDtypeStruct(mean.shape, F32),
+            jax.ShapeDtypeStruct((CLEV, 256), F32),
+        ),
+        in_specs=[VMEM] * 3,
+        out_specs=(HBM, VMEM),
+        scratch_shapes=[pltpu.SemaphoreType.DMA(())],
+        compiler_params=pltpu.CompilerParams(vmem_limit_bytes=8 << 20),
+        name="finish",
+    )(mean, rows, jnp.asarray(slot_table()))
 
 
 def shards(tracer, wind_x, wind_y, drops, owner, counts, collision, growth):
@@ -769,7 +808,7 @@
     drops_next, heat, echo = microphysics(
         sorted_counts, start, cell_forcing, pair_coef, growth_col, unsort, quadratic, linear, constant
     )
-    tracer_next, power = coupling(state, heat, echo, sender)
+    tracer_next, power = finish(*coupling(state, heat, echo, sender))
     return (tracer_next, drops_next.transpose(1, 0, 2), power)
 
 

time: 67 us -> 68.6 us (1.024)
  Pallas kernels: 63.7 us -> 66.7 us
  local copies, waits for them, and re-layouts: 1.45 us -> 0.03 us
    pallas_call x1, Pallas kernels: 24.3 us -> 26.1 us  [dynamics(): pl.pallas_call(dynamics_kernel, out_shape=(jax.ShapeDtypeStruct(shape, F3...]
    pallas_call x0 -> x1, Pallas kernels: none -> 1.45 us  [finish(): pl.pallas_call(finish_kernel, out_shape=(jax.ShapeDtypeStruct(mean.shape,...]
    unnamed x10 -> x8, local copies, waits for them, and re-layouts: 1.45 us -> 0.03 us
where the time goes in v6:
time: 68.6 us; the launch traced here: 67.5 us
  Pallas kernels  66.7 us (97%)
  between operations  0.72 us (1%)
    pallas_call x1, Pallas kernels, coupling(): pl.pallas_call(coupling_kernel, out_shape=(jax.ShapeDtypeStruct(state.sha...  32.6 us
    pallas_call x1, Pallas kernels, dynamics(): pl.pallas_call(dynamics_kernel, out_shape=(jax.ShapeDtypeStruct(shape, F3...  26.1 us
    pallas_call x1, Pallas kernels, microphysics(): pl.pallas_call(micro_kernel, out_shape=(jax.ShapeDtypeStruct((BINS, COLS,...  6.65 us
    pallas_call x1, Pallas kernels, finish(): pl.pallas_call(finish_kernel, out_shape=(jax.ShapeDtypeStruct(mean.shape,...  1.45 us

profile of v6, /device:TPU:0, one launch (start us, length us, event | category | flops | bytes accessed | tf_op | source)
XLA Modules:
  0.0 67.5 jit_solution(7895185776400533945)
XLA Ops:
  0.6 0.0 copy-start.2
  0.6 26.1 %dynamics.1 = (f32[72,8,256]{2,1,0:T(8,128)S(1)}, f32[128,256]{1,0:T(8,128)S(1)}, bf16[48,576]{1,0:T(8,128)(2,1)S(1)}, f32[40,128]{1,0:T(8,128)S(1)}, f32[10240,...) custom-call(f32[72,8,256]{2,1,0:T(8,128)} %tracer_h.1, ...), custom_call_target="tpu_custom_call" | custom-call | tf_op jit(solution)/shard_map/dynamics/pallas_call | solution.py:520
  26.7 0.0 copy-done.2
  26.7 0.0 copy-start
  26.7 0.0 copy-start.3
  26.8 0.0 copy-start.1
  26.8 6.7 %microphysics.1 = (bf16[33,128,256]{2,1,0:T(8,128)(2,1)}, bf16[128,128]{1,0:T(8,128)(2,1)S(1)}, f32[128,128]{1,0:T(8,128)S(1)}) custom-call(s32[1,128]{1,0:T(1,128)S(1)} %get-tuple-element.22.counts, f32[10240,128]{1,0:T(8,128)S(1)} %get-tuple-element.23.start, f32[128,256]{1,0:T(8,128)S(1)} %get-tuple-element.24.cell_forcing, ...), custom_call_target="tpu_custom_call" | custom-call | tf_op jit(solution)/shard_map/microphysics/pallas_call | solution.py:645
  33.4 0.0 copy-done
  33.4 0.0 copy-done.3
  33.5 32.6 %coupling.1 = (f32[72,8,256]{2,1,0:T(8,128)S(1)}, f32[128,128]{1,0:T(8,128)S(1)}) custom-call(f32[72,8,256]{2,1,0:T(8,128)S(1)} %get-tuple-element.21.state, bf16[128,128]{1,0:T(8,128)(2,1)S(1)} %get-tuple-element.31.heat, f32[128,128]{1,0:T(8,128)S(1)} %get-tuple-element.32.echo, bf16[128,256]{1,0:T(8,128)(2,1)S(1)} %get-tuple-element.33.sender, ...), custom_call_target="tpu_custom_call" | custom-call | tf_op jit(solution)/shard_map/coupling/pallas_call | solution.py:745
  66.0 0.0 copy-done.1
  66.0 1.4 %finish.1 = (f32[72,8,256]{2,1,0:T(8,128)}, f32[16,256]{1,0:T(8,128)}) custom-call(f32[72,8,256]{2,1,0:T(8,128)S(1)} %get-tuple-element.34.mean, f32[128,128]{1,0:T(8,128)S(1)} %get-tuple-element.35.rows, bf16[256,256]{1,0:T(8,128)(2,1)S(1)} %copy-done.1), custom_call_target="tpu_custom_call" | custom-call | tf_op jit(solution)/shard_map/finish/pallas_call | solution.py:789
Async XLA Ops:
  0.6 26.1 %copy-start.2 = (bf16[256,128]{1,0:T(8,128)(2,1)S(1)}, bf16[256,128]{1,0:T(8,128)(2,1)}, u32[]{:S(2)}) copy-start(bf16[256,128]{1,0:T(8,128)(2,1)} %constant.29.clone.group) | copy-start | bytes 196612
  26.7 6.7 %copy-start = (bf16[576,64]{1,0:T(8,128)(2,1)S(1)}, bf16[576,64]{1,0:T(8,128)(2,1)}, u32[]{:S(2)}) copy-start(bf16[576,64]{1,0:T(8,128)(2,1)} %constant.30.clone.heating) | copy-start | bytes 221188
  26.7 6.7 %copy-start.3 = (bf16[64,256]{1,0:T(8,128)(2,1)S(1)}, bf16[64,256]{1,0:T(8,128)(2,1)}, u32[]{:S(2)}) copy-start(bf16[64,256]{1,0:T(8,128)(2,1)} %constant.31.clone.spread) | copy-start | bytes 98308
  26.8 39.3 %copy-start.1 = (bf16[256,256]{1,0:T(8,128)(2,1)S(1)}, bf16[256,256]{1,0:T(8,128)(2,1)}, u32[]{:S(2)}) copy-start(bf16[256,256]{1,0:T(8,128)(2,1)} %constant.32.clone.slots) | copy-start | bytes 393220

commit v7 on v6

--- a/solution.py
+++ b/solution.py
@@ -30,7 +30,7 @@
 DT_PHYS = 0.5
 BATCH = 32
 ROWS = 40
-EARLY = 1
+EARLY = 3
 
 
 def gll_tables():
@@ -242,7 +242,9 @@
         return low, high
 
     zero = jnp.zeros((8, 128), F32)
-    low, high = lax.fori_loop(0, 9, one, (zero, zero))
+    low, high = lax.fori_loop(
+        0, 3, lambda n, edges: one(3 * n + 2, one(3 * n + 1, one(3 * n, edges))), (zero, zero)
+    )
     packs[0] = pltpu.roll(low, 63, 1)
     packs[1] = pltpu.roll(high, 64, 1)
     for half in range(2):
@@ -310,8 +312,10 @@
             at = pl.multiple_of(half * PTS + i * 64, 64)
             x = field[pl.ds(at, 64), :].reshape(8, 8, 128)
             lev = pl.multiple_of(half * LEV + i * 8, 8)
-            above = jnp.broadcast_to(got_rows[0, pl.ds(lev, 8), :][:, None, :], (8, 8, 128))
-            below = jnp.broadcast_to(got_rows[1, pl.ds(lev, 8), :][:, None, :], (8, 8, 128))
+            above, below = (
+                jnp.stack([got_rows[side, pl.ds(lev + k, 8, stride=0), :] for k in range(8)])
+                for side in range(2)
+            )
             other = jnp.where(is3, pltpu.roll(x, 7, 1), jnp.where(is4, pltpu.roll(x, 1, 1), x))
             other = jnp.where(edge_row, jnp.where(upper, above, below), other)
             means.append(0.5 * (x + other))
@@ -329,7 +333,9 @@
         use(i, done)
         return pltpu.roll(left_c, 120, 1), pltpu.roll(right_c, 120, 1)
 
-    lax.fori_loop(0, 9, one, (left_halo, right_halo))
+    halos = (left_halo, right_halo)
+    for i in range(9):
+        halos = one(i, halos)
 
 
 def chunk_of(ref, i):

time: 68.6 us -> 63 us (0.918)
  Pallas kernels: 66.7 us -> 61.1 us
    pallas_call x1, Pallas kernels: 26.1 us -> 21.7 us  [dynamics(): pl.pallas_call(dynamics_kernel, out_shape=(jax.ShapeDtypeStruct(shape, F3...]
    pallas_call x1, Pallas kernels: 32.6 us -> 31.3 us  [coupling(): pl.pallas_call(coupling_kernel, out_shape=(jax.ShapeDtypeStruct(state.sha...]
where the time goes in v7:
time: 63 us; the launch traced here: 61.9 us
  Pallas kernels  61.1 us (97%)
  between operations  0.72 us (1%)
    pallas_call x1, Pallas kernels, coupling(): pl.pallas_call(coupling_kernel, out_shape=(jax.ShapeDtypeStruct(state.sha...  31.3 us
    pallas_call x1, Pallas kernels, dynamics(): pl.pallas_call(dynamics_kernel, out_shape=(jax.ShapeDtypeStruct(shape, F3...  21.7 us
    pallas_call x1, Pallas kernels, microphysics(): pl.pallas_call(micro_kernel, out_shape=(jax.ShapeDtypeStruct((BINS, COLS,...  6.65 us
    pallas_call x1, Pallas kernels, finish(): pl.pallas_call(finish_kernel, out_shape=(jax.ShapeDtypeStruct(mean.shape,...  1.45 us

profile of v7, /device:TPU:0, one launch (start us, length us, event | category | flops | bytes accessed | tf_op | source)
XLA Modules:
  0.0 61.9 jit_solution(10865987028911407766)
XLA Ops:
  0.6 0.0 copy-start.2
  0.6 21.7 %dynamics.1 = (f32[72,8,256]{2,1,0:T(8,128)S(1)}, f32[128,256]{1,0:T(8,128)S(1)}, bf16[48,576]{1,0:T(8,128)(2,1)S(1)}, f32[40,128]{1,0:T(8,128)S(1)}, f32[10240,...) custom-call(f32[72,8,256]{2,1,0:T(8,128)} %tracer_h.1, ...), custom_call_target="tpu_custom_call" | custom-call | tf_op jit(solution)/shard_map/dynamics/pallas_call | solution.py:526
  22.4 0.0 copy-done.2
  22.4 0.0 copy-start
  22.4 0.0 copy-start.3
  22.4 0.0 copy-start.1
  22.4 6.7 %microphysics.1 = (bf16[33,128,256]{2,1,0:T(8,128)(2,1)}, bf16[128,128]{1,0:T(8,128)(2,1)S(1)}, f32[128,128]{1,0:T(8,128)S(1)}) custom-call(s32[1,128]{1,0:T(1,128)S(1)} %get-tuple-element.22.counts, f32[10240,128]{1,0:T(8,128)S(1)} %get-tuple-element.23.start, f32[128,256]{1,0:T(8,128)S(1)} %get-tuple-element.24.cell_forcing, ...), custom_call_target="tpu_custom_call" | custom-call | tf_op jit(solution)/shard_map/microphysics/pallas_call | solution.py:651
  29.1 0.0 copy-done
  29.1 0.0 copy-done.3
  29.1 31.3 %coupling.1 = (f32[72,8,256]{2,1,0:T(8,128)S(1)}, f32[128,128]{1,0:T(8,128)S(1)}) custom-call(f32[72,8,256]{2,1,0:T(8,128)S(1)} %get-tuple-element.21.state, bf16[128,128]{1,0:T(8,128)(2,1)S(1)} %get-tuple-element.31.heat, f32[128,128]{1,0:T(8,128)S(1)} %get-tuple-element.32.echo, bf16[128,256]{1,0:T(8,128)(2,1)S(1)} %get-tuple-element.33.sender, ...), custom_call_target="tpu_custom_call" | custom-call | tf_op jit(solution)/shard_map/coupling/pallas_call | solution.py:751
  60.4 0.0 copy-done.1
  60.4 1.4 %finish.1 = (f32[72,8,256]{2,1,0:T(8,128)}, f32[16,256]{1,0:T(8,128)}) custom-call(f32[72,8,256]{2,1,0:T(8,128)S(1)} %get-tuple-element.34.mean, f32[128,128]{1,0:T(8,128)S(1)} %get-tuple-element.35.rows, bf16[256,256]{1,0:T(8,128)(2,1)S(1)} %copy-done.1), custom_call_target="tpu_custom_call" | custom-call | tf_op jit(solution)/shard_map/finish/pallas_call | solution.py:795
Async XLA Ops:
  0.6 21.8 %copy-start.2 = (bf16[256,128]{1,0:T(8,128)(2,1)S(1)}, bf16[256,128]{1,0:T(8,128)(2,1)}, u32[]{:S(2)}) copy-start(bf16[256,128]{1,0:T(8,128)(2,1)} %constant.29.clone.group) | copy-start | bytes 196612
  22.4 6.7 %copy-start = (bf16[576,64]{1,0:T(8,128)(2,1)S(1)}, bf16[576,64]{1,0:T(8,128)(2,1)}, u32[]{:S(2)}) copy-start(bf16[576,64]{1,0:T(8,128)(2,1)} %constant.30.clone.heating) | copy-start | bytes 221188
  22.4 6.7 %copy-start.3 = (bf16[64,256]{1,0:T(8,128)(2,1)S(1)}, bf16[64,256]{1,0:T(8,128)(2,1)}, u32[]{:S(2)}) copy-start(bf16[64,256]{1,0:T(8,128)(2,1)} %constant.31.clone.spread) | copy-start | bytes 98308
  22.4 38.0 %copy-start.1 = (bf16[256,256]{1,0:T(8,128)(2,1)S(1)}, bf16[256,256]{1,0:T(8,128)(2,1)}, u32[]{:S(2)}) copy-start(bf16[256,256]{1,0:T(8,128)(2,1)} %constant.32.clone.slots) | copy-start | bytes 393220

commit v8 on v7

--- a/solution.py
+++ b/solution.py
@@ -242,9 +242,9 @@
         return low, high
 
     zero = jnp.zeros((8, 128), F32)
-    low, high = lax.fori_loop(
-        0, 3, lambda n, edges: one(3 * n + 2, one(3 * n + 1, one(3 * n, edges))), (zero, zero)
-    )
+    low, high = zero, zero
+    for i in range(9):
+        low, high = one(i, (low, high))
     packs[0] = pltpu.roll(low, 63, 1)
     packs[1] = pltpu.roll(high, 64, 1)
     for half in range(2):
@@ -375,10 +375,12 @@
         pltpu.make_async_copy(source, target, loads.at[n])
         for n, (source, target) in enumerate(zip(sources[3:], targets[3:]))
     ]
-    for copy in fetch[0:2] + thirds[0] + thirds[1] + thirds[2] + fetch[2:]:
+    for copy in thirds[0] + fetch[0:2]:
         copy.start()
     for to in around:
         pl.semaphore_signal(barrier, inc=1, device_id=to, device_id_type=MESH)
+    for copy in thirds[1] + thirds[2] + fetch[2:]:
+        copy.start()
     for copy in fetch[0:2]:
         copy.wait()
     for n in range(3):
@@ -572,15 +574,32 @@
     def place(p, b, half):
         return column_rows(p * BATCH + b, half)
 
-    def substep(s, p):
+    def advance(col, b, active=None):
+        olds = [cloud[column_rows(col, half), :] for half in range(2)]
+        grown = [olds[half] + grow[b, half] for half in range(2)]
+        change = jnp.dot(pair_coef[...], pairs_of(grown, doubled.at[b]), preferred_element_type=F32)
+        for half in range(2):
+            moved = grown[half] + DT_CRM * change[0:ROWS, half * 128 : (half + 1) * 128]
+            if active is not None:
+                moved = jnp.where(active, moved, olds[half])
+            cloud[column_rows(col, half), :] = moved
+
+    def substep(_, p):
         for b in range(BATCH):
-            active = s < counts[0, p * BATCH + b]
-            olds = [cloud[place(p, b, half), :] for half in range(2)]
-            grown = [olds[half] + grow[b, half] for half in range(2)]
-            change = jnp.dot(pair_coef[...], pairs_of(grown, doubled.at[b]), preferred_element_type=F32)
-            for half in range(2):
-                moved = grown[half] + DT_CRM * change[0:ROWS, half * 128 : (half + 1) * 128]
-                cloud[place(p, b, half), :] = jnp.where(active, moved, olds[half])
+            advance(p * BATCH + b, b)
+        return p
+
+    def ragged(s, p):
+        def part(h, _):
+            @pl.when(s < counts[0, p * BATCH + h * 16])
+            def _():
+                for k in range(16):
+                    col = p * BATCH + h * 16 + k
+                    advance(col, h * 16 + k, s < counts[0, col])
+
+            return 0
+
+        lax.fori_loop(0, BATCH // 16, part, 0)
         return p
 
     def batch(p, _):
@@ -600,7 +619,9 @@
                 grow[b, half] = add
                 moved = olds[half] + add + DT_CRM * change
                 cloud[place(p, b, half), :] = jnp.where(active, moved, olds[half])
-        lax.fori_loop(1, counts[0, p * BATCH], substep, p)
+        common = jnp.maximum(counts[0, p * BATCH + BATCH - 1], 1)
+        lax.fori_loop(1, common, substep, p)
+        lax.fori_loop(common, counts[0, p * BATCH], ragged, p)
         for half in range(2):
             at = slice(half * 128, (half + 1) * 128)
             for eight in range(BATCH // 8):

time: 63 us -> 61.4 us (0.975)
  Pallas kernels: 61.1 us -> 59.5 us
    pallas_call x1, Pallas kernels: 31.3 us -> 10.9 us  [coupling(): pl.pallas_call(coupling_kernel, out_shape=(jax.ShapeDtypeStruct(state.sha...]
    pallas_call x1, Pallas kernels: 6.65 us -> 25.9 us  [microphysics(): pl.pallas_call(micro_kernel, out_shape=(jax.ShapeDtypeStruct((BINS, COLS,...]
where the time goes in v8:
time: 61.4 us; the launch traced here: 60.2 us
  Pallas kernels  59.5 us (97%)
  between operations  0.72 us (1%)
    pallas_call x1, Pallas kernels, microphysics(): pl.pallas_call(micro_kernel, out_shape=(jax.ShapeDtypeStruct((BINS, COLS,...  25.9 us
    pallas_call x1, Pallas kernels, dynamics(): pl.pallas_call(dynamics_kernel, out_shape=(jax.ShapeDtypeStruct(shape, F3...  21.3 us
    pallas_call x1, Pallas kernels, coupling(): pl.pallas_call(coupling_kernel, out_shape=(jax.ShapeDtypeStruct(state.sha...  10.9 us
    pallas_call x1, Pallas kernels, finish(): pl.pallas_call(finish_kernel, out_shape=(jax.ShapeDtypeStruct(mean.shape,...  1.45 us

profile of v8, /device:TPU:0, one launch (start us, length us, event | category | flops | bytes accessed | tf_op | source)
XLA Modules:
  0.0 60.2 jit_solution(9869465381249277181)
XLA Ops:
  0.6 0.0 copy-start.2
  0.6 21.3 %dynamics.1 = (f32[72,8,256]{2,1,0:T(8,128)S(1)}, f32[128,256]{1,0:T(8,128)S(1)}, bf16[48,576]{1,0:T(8,128)(2,1)S(1)}, f32[40,128]{1,0:T(8,128)S(1)}, f32[10240,...) custom-call(f32[72,8,256]{2,1,0:T(8,128)} %tracer_h.1, ...), custom_call_target="tpu_custom_call" | custom-call | tf_op jit(solution)/shard_map/dynamics/pallas_call | solution.py:528
  22.0 0.0 copy-done.2
  22.0 0.0 copy-start
  22.0 0.0 copy-start.3
  22.0 0.0 copy-start.1
  22.0 25.9 %microphysics.1 = (bf16[33,128,256]{2,1,0:T(8,128)(2,1)}, bf16[128,128]{1,0:T(8,128)(2,1)S(1)}, f32[128,128]{1,0:T(8,128)S(1)}) custom-call(s32[1,128]{1,0:T(1,128)S(1)} %get-tuple-element.22.counts, f32[10240,128]{1,0:T(8,128)S(1)} %get-tuple-element.23.start, f32[128,256]{1,0:T(8,128)S(1)} %get-tuple-element.24.cell_forcing, ...), custom_call_target="tpu_custom_call" | custom-call | tf_op jit(solution)/shard_map/microphysics/pallas_call | solution.py:672
  47.9 0.0 copy-done
  47.9 0.0 copy-done.3
  47.9 10.9 %coupling.1 = (f32[72,8,256]{2,1,0:T(8,128)S(1)}, f32[128,128]{1,0:T(8,128)S(1)}) custom-call(f32[72,8,256]{2,1,0:T(8,128)S(1)} %get-tuple-element.21.state, bf16[128,128]{1,0:T(8,128)(2,1)S(1)} %get-tuple-element.31.heat, f32[128,128]{1,0:T(8,128)S(1)} %get-tuple-element.32.echo, bf16[128,256]{1,0:T(8,128)(2,1)S(1)} %get-tuple-element.33.sender, ...), custom_call_target="tpu_custom_call" | custom-call | tf_op jit(solution)/shard_map/coupling/pallas_call | solution.py:772
  58.8 0.0 copy-done.1
  58.8 1.4 %finish.1 = (f32[72,8,256]{2,1,0:T(8,128)}, f32[16,256]{1,0:T(8,128)}) custom-call(f32[72,8,256]{2,1,0:T(8,128)S(1)} %get-tuple-element.34.mean, f32[128,128]{1,0:T(8,128)S(1)} %get-tuple-element.35.rows, bf16[256,256]{1,0:T(8,128)(2,1)S(1)} %copy-done.1), custom_call_target="tpu_custom_call" | custom-call | tf_op jit(solution)/shard_map/finish/pallas_call | solution.py:816
Async XLA Ops:
  0.6 21.3 %copy-start.2 = (bf16[256,128]{1,0:T(8,128)(2,1)S(1)}, bf16[256,128]{1,0:T(8,128)(2,1)}, u32[]{:S(2)}) copy-start(bf16[256,128]{1,0:T(8,128)(2,1)} %constant.29.clone.group) | copy-start | bytes 196612
  22.0 25.9 %copy-start = (bf16[576,64]{1,0:T(8,128)(2,1)S(1)}, bf16[576,64]{1,0:T(8,128)(2,1)}, u32[]{:S(2)}) copy-start(bf16[576,64]{1,0:T(8,128)(2,1)} %constant.30.clone.heating) | copy-start | bytes 221188
  22.0 25.9 %copy-start.3 = (bf16[64,256]{1,0:T(8,128)(2,1)S(1)}, bf16[64,256]{1,0:T(8,128)(2,1)}, u32[]{:S(2)}) copy-start(bf16[64,256]{1,0:T(8,128)(2,1)} %constant.31.clone.spread) | copy-start | bytes 98308
  22.0 36.8 %copy-start.1 = (bf16[256,256]{1,0:T(8,128)(2,1)S(1)}, bf16[256,256]{1,0:T(8,128)(2,1)}, u32[]{:S(2)}) copy-start(bf16[256,256]{1,0:T(8,128)(2,1)} %constant.32.clone.slots) | copy-start | bytes 393220
